TPU v7x, 32 devices: a whole 2x2x4 slice. The times are simulated.
32 devices in a mesh: groups: 2 (over y), hosts: 4 (over z), mp: 4 (over x, core).
Axes of the slice: x: 2, y: 2, z: 4, core: 2. Of those that a mesh axis runs over, the one named last changes fastest.
Arguments:
- hidden: bfloat16 [256, 4096], P(('groups', 'hosts'), 'mp'), parts along dimension 0, may hold values from -6 to 6
- base_query_projection: bfloat16 [256, 4096], P(('groups', 'hosts'), 'mp'), parts along dimension 0, may hold values from -160 to 160
- base_key_projection: bfloat16 [256, 4096], P(('groups', 'hosts'), 'mp'), parts along dimension 0, may hold values from -6 to 6
- base_value_projection: bfloat16 [256, 4096], P(('groups', 'hosts'), 'mp'), parts along dimension 0, may hold values from -6 to 6
- adapter_input_factors: bfloat16 [8, 4096, 128], P(('groups', 'hosts'), 'mp'), parts along dimension 0, may hold values from -0.09375 to 0.09375
- adapter_output_factors: bfloat16 [8, 2, 64, 4096], P(('groups', 'hosts'), None, None, 'mp'), parts along dimension 0, may hold values from -0.75 to 0.75
- statement_prefix_cache: bfloat16 [32, 2, 128, 4096], P(('groups', 'hosts'), None, None, 'mp'), parts along dimension 0, may hold values from -6 to 6
- generated_token_cache: bfloat16 [256, 2, 8, 4096], P(('groups', 'hosts'), None, None, 'mp'), parts along dimension 0, may hold values from -6 to 6
- attempt_theorem_index: int32 [256], P(('groups', 'hosts')), parts along dimension 0, may hold values from 0 to 3, as said below
- host_live_count: int32 [8], P(('groups', 'hosts')), parts along dimension 0, may hold values from 8 to 32, as said below
- adapter_pool_row: int32 [8], P('groups'), parts along dimension 0, may hold values from 0 to 3, as said below
- prefix_pool_row: int32 [8, 4], P('groups'), parts along dimension 0, may hold values from 0 to 15, as said below
- prefix_block_count: int32 [8], P('groups'), parts along dimension 0, may hold values from 1 to 4
Outputs:
- attended: bfloat16 [256, 4096], P(('groups', 'hosts'), 'mp'), parts along dimension 0
- key_rows: bfloat16 [256, 4096], P(('groups', 'hosts'), 'mp'), parts along dimension 0
- value_rows: bfloat16 [256, 4096], P(('groups', 'hosts'), 'mp'), parts along dimension 0
There are 2 independent parts, one for each index of `groups`. A program takes and returns all parts, laid end to end along the dimension named above; each array names one. Nothing has to cross between parts.
Inputs may be any that keep to these rules, and one draw needn't show every extreme that they name: `attempt_theorem_index`: among the live attempts of one host, at most 8 name theorems whose adapter lies on any one host, and for each block index at most 8 name theorems whose block of that index lies on any one host. One host holds the adapters named by 8 live attempts of every host, and one host holds the first blocks named by 8 live attempts of every host. `host_live_count`: rows at or above a host's count are empty; some host has all 32 rows live. `adapter_pool_row`: all entries differ; pool row p lies on host p. `prefix_pool_row`: all entries differ; pool row p lies on host p // 4.
All inputs are finite; a program needn't handle non-finite values.
Results may differ from a plain program's by a relative error of at most 0.011.
Values may be sent and summed in bfloat16 or wider, within the bound.
No kernel may reach another device: no remote copies, remote signals or barrier semaphores. Data moves between devices by JAX's collectives and lax.ppermute only.
A program may use at most 64 MiB of HBM per device.

v0:
```python
import jax
import jax.numpy as jnp
from jax import lax
from jax.sharding import PartitionSpec as P

HEAD_SIZE = 128
ADAPTER_RANK = 64
BLK = 128
PBLK = 4


ADAPTER_SCALE = 0.5
ROPE_BASE = 10000.0
NEG_FILL = -1e30


def rotate(values, position):
    shaped = values.reshape(values.shape[:-1] + (-1, HEAD_SIZE))
    halfway = HEAD_SIZE // 2
    frequency = ROPE_BASE ** (-(jnp.arange(halfway, dtype=jnp.float32) * (2.0 / HEAD_SIZE)))
    angles = position.astype(jnp.float32)[..., None] * frequency
    cosine = jnp.cos(angles)[..., None, :]
    sine_part = jnp.sin(angles)[..., None, :]
    first_half = shaped[..., :halfway]
    second = shaped[..., halfway:]
    turned = jnp.concatenate(
        [first_half * cosine - second * sine_part, second * cosine + first_half * sine_part],
        axis=-1,
    )
    return turned.reshape(values.shape)


def lookup_table(source_table, wanted):
    matches = wanted[:, None] == jnp.arange(source_table.shape[0], dtype=jnp.int32)[None, :]
    if source_table.ndim == 1:
        return jnp.sum(jnp.where(matches, source_table[None, :], 0), axis=1)
    return jnp.sum(jnp.where(matches[:, :, None], source_table[None, :, :], 0), axis=1)


def route_matrix(destination, validity, capacity, host_total):
    ordinal = jnp.arange(destination.shape[0], dtype=jnp.int32)
    earlier = (
        (destination[:, None] == destination[None, :])
        & validity[None, :]
        & (ordinal[None, :] < ordinal[:, None])
    )
    ranking = jnp.sum(earlier.astype(jnp.int32), axis=1)
    target = destination * capacity + ranking
    places = jnp.arange(host_total * capacity, dtype=jnp.int32)
    return ((places[:, None] == target[None, :]) & validity[None, :]).astype(jnp.bfloat16)


def pack_rows(router, payload):
    return jnp.dot(router, payload, preferred_element_type=jnp.float32).astype(jnp.bfloat16)


def attend_local(queries, chosen, statement_prefix_cache):
    head_count = queries.shape[-1] // HEAD_SIZE
    blocks = statement_prefix_cache.shape[0]
    block_keys = statement_prefix_cache[:, 0].reshape(
        blocks, statement_prefix_cache.shape[2], head_count, HEAD_SIZE
    )
    block_values = statement_prefix_cache[:, 1].reshape(
        blocks, statement_prefix_cache.shape[2], head_count, HEAD_SIZE
    )
    shaped = queries.reshape(queries.shape[:-1] + (head_count, HEAD_SIZE))
    scores = jnp.einsum(
        "nchd,bthd->ncbht", shaped, block_keys, preferred_element_type=jnp.float32
    ) * HEAD_SIZE ** (-0.5)
    chosen_mask = (chosen > 0)[:, :, :, None, None]
    masked = jnp.where(chosen_mask, scores, NEG_FILL)
    top_score = jnp.max(masked, axis=(2, 4))
    weights = jnp.where(chosen_mask, jnp.exp(masked - top_score[:, :, None, :, None]), 0.0)
    totals = jnp.sum(weights, axis=(2, 4))
    mixed_rows = jnp.einsum(
        "ncbht,bthd->nchd",
        weights.astype(jnp.bfloat16),
        block_values,
        preferred_element_type=jnp.float32,
    )
    return (mixed_rows.reshape(queries.shape), top_score, totals)


def body(
    hidden,
    base_query_projection,
    base_key_projection,
    base_value_projection,
    adapter_input_factors,
    adapter_output_factors,
    statement_prefix_cache,
    generated_token_cache,
    attempt_theorem_index,
    host_live_count,
    adapter_pool_row,
    prefix_pool_row,
    prefix_block_count,
):
    host_total = lax.axis_size("hosts")
    attempts = hidden.shape[0]
    capacity = max(1, attempts // host_total)
    owner_held_rows = adapter_input_factors.shape[0]
    local_blocks = statement_prefix_cache.shape[0]
    row_width = base_query_projection.shape[1]
    head_count = row_width // HEAD_SIZE
    ordinal = jnp.arange(attempts, dtype=jnp.int32)
    living = ordinal < host_live_count[0]
    adapter_rows = lookup_table(adapter_pool_row, attempt_theorem_index)
    block_rows = lookup_table(prefix_pool_row, attempt_theorem_index)
    block_counts = lookup_table(prefix_block_count, attempt_theorem_index)
    position = BLK * block_counts + generated_token_cache.shape[2]
    adapter_router = route_matrix(adapter_rows // owner_held_rows, living, capacity, host_total)
    adapter_pick = (
        adapter_rows[:, None] % owner_held_rows
        == jnp.arange(owner_held_rows, dtype=jnp.int32)[None, :]
    ).astype(jnp.bfloat16)
    sent_hidden = pack_rows(adapter_router, hidden).reshape(host_total, capacity, hidden.shape[1])
    sent_pick = pack_rows(adapter_router, adapter_pick).reshape(
        host_total, capacity, owner_held_rows
    )
    incoming_rows = lax.all_to_all(sent_hidden, "hosts", split_axis=0, concat_axis=0, tiled=True)
    pick_in = lax.all_to_all(sent_pick, "hosts", split_axis=0, concat_axis=0, tiled=True)
    projected_rows = jnp.einsum(
        "xjp,epk->xjek", incoming_rows, adapter_input_factors, preferred_element_type=jnp.float32
    )
    partial_rank = jnp.sum(projected_rows * pick_in.astype(jnp.float32)[..., None], axis=2)
    rank_rows = lax.psum(partial_rank, "mp").astype(jnp.bfloat16)
    spread_rows = rank_rows[:, :, None, :] * pick_in[..., None]
    query_correction = jnp.einsum(
        "exqw,qwf->exf",
        spread_rows[..., :ADAPTER_RANK],
        adapter_output_factors[:, 0],
        preferred_element_type=jnp.float32,
    )
    value_correction = jnp.einsum(
        "exqw,qwf->exf",
        spread_rows[..., ADAPTER_RANK:],
        adapter_output_factors[:, 1],
        preferred_element_type=jnp.float32,
    )
    adapter_corrections = (
        jnp.concatenate([query_correction, value_correction], axis=-1) * ADAPTER_SCALE
    ).astype(jnp.bfloat16)
    returned = lax.all_to_all(adapter_corrections, "hosts", split_axis=0, concat_axis=0, tiled=True)
    adapter_corrections = jnp.dot(
        adapter_router.T,
        returned.reshape(host_total * capacity, 2 * row_width),
        preferred_element_type=jnp.float32,
    )
    query_rows = rotate(
        base_query_projection.astype(jnp.float32) + adapter_corrections[:, :row_width], position
    ).astype(jnp.bfloat16)
    value_rows = (
        base_value_projection.astype(jnp.float32) + adapter_corrections[:, row_width:]
    ).astype(jnp.bfloat16)
    key_rows = rotate(base_key_projection.astype(jnp.float32), position).astype(jnp.bfloat16)
    requests = []
    for block_index in range(PBLK):
        wanted = living & (block_index < block_counts)
        holder = block_rows[:, block_index]
        router = route_matrix(holder // local_blocks, wanted, capacity, host_total)
        block_pick = (
            holder[:, None] % local_blocks == jnp.arange(local_blocks, dtype=jnp.int32)[None, :]
        ).astype(jnp.bfloat16)
        sent_queries = pack_rows(router, query_rows).reshape(host_total, capacity, row_width)
        sent_blocks = pack_rows(router, block_pick).reshape(host_total, capacity, local_blocks)
        requests.append((router, wanted, sent_queries, sent_blocks))
    partials = []
    for request in requests:
        answer_mixed_rows, answer_top_score, answer_totals = attend_local(
            lax.all_to_all(request[2], "hosts", split_axis=0, concat_axis=0, tiled=True),
            lax.all_to_all(request[3], "hosts", split_axis=0, concat_axis=0, tiled=True),
            statement_prefix_cache,
        )
        partials.append(
            (
                lax.all_to_all(answer_mixed_rows, "hosts", split_axis=0, concat_axis=0, tiled=True),
                lax.all_to_all(answer_top_score, "hosts", split_axis=0, concat_axis=0, tiled=True),
                lax.all_to_all(answer_totals, "hosts", split_axis=0, concat_axis=0, tiled=True),
            )
        )
    entries = []
    for block_index in range(PBLK):
        router, wanted = (requests[block_index][0], requests[block_index][1])
        mixed_rows, top_score, totals = partials[block_index]
        back_router = router.T.astype(jnp.float32)
        flat_mixed = jnp.dot(
            back_router,
            mixed_rows.reshape(host_total * capacity, row_width),
            precision=lax.Precision.HIGHEST,
        )
        flat_top = jnp.dot(
            back_router,
            top_score.reshape(host_total * capacity, head_count),
            precision=lax.Precision.HIGHEST,
        )
        flat_totals = jnp.dot(
            back_router,
            totals.reshape(host_total * capacity, head_count),
            precision=lax.Precision.HIGHEST,
        )
        flat_top = jnp.where(wanted[:, None], flat_top, NEG_FILL)
        entries.append((flat_mixed, flat_top, flat_totals))
    shaped_query = query_rows.reshape(attempts, head_count, HEAD_SIZE)
    own_keys = jnp.concatenate([generated_token_cache[:, 0], key_rows[:, None, :]], axis=1).reshape(
        attempts, -1, head_count, HEAD_SIZE
    )
    own_values = jnp.concatenate(
        [generated_token_cache[:, 1], value_rows[:, None, :]], axis=1
    ).reshape(attempts, -1, head_count, HEAD_SIZE)
    own_scores = jnp.einsum(
        "ahd,athd->aht", shaped_query, own_keys, preferred_element_type=jnp.float32
    ) * HEAD_SIZE ** (-0.5)
    own_top = jnp.max(own_scores, axis=2)
    own_weights = jnp.exp(own_scores - own_top[..., None])
    own_totals = jnp.sum(own_weights, axis=2)
    own_mixed = jnp.einsum(
        "aht,athd->ahd",
        own_weights.astype(jnp.bfloat16),
        own_values,
        preferred_element_type=jnp.float32,
    )
    overall = own_top
    for flat_mixed, flat_top, flat_totals in entries:
        overall = jnp.maximum(overall, flat_top)
    own_factor = jnp.exp(own_top - overall)
    numerator = own_mixed * own_factor[..., None]
    denominator = own_totals * own_factor
    for flat_mixed, flat_top, flat_totals in entries:
        factor = jnp.exp(flat_top - overall)
        numerator = (
            numerator + flat_mixed.reshape(attempts, head_count, HEAD_SIZE) * factor[..., None]
        )
        denominator = denominator + flat_totals * factor
    attended = (numerator / denominator[..., None]).reshape(attempts, row_width)
    live_rows = living[:, None]
    return (
        jnp.where(live_rows, attended, 0.0).astype(jnp.bfloat16),
        jnp.where(live_rows, key_rows, 0.0),
        jnp.where(live_rows, value_rows, 0.0),
    )


def solution(mesh):
    placed = (
        P(("groups", "hosts"), "mp"),
        P(("groups", "hosts"), "mp"),
        P(("groups", "hosts"), "mp"),
        P(("groups", "hosts"), "mp"),
        P(("groups", "hosts"), "mp", None),
        P(("groups", "hosts"), None, None, "mp"),
        P(("groups", "hosts"), None, None, "mp"),
        P(("groups", "hosts"), None, None, "mp"),
        P(("groups", "hosts")),
        P(("groups", "hosts")),
        P("groups"),
        P("groups", None),
        P("groups"),
    )
    return jax.shard_map(
        body,
        mesh=mesh,
        in_specs=placed,
        out_specs=(
            P(("groups", "hosts"), "mp"),
            P(("groups", "hosts"), "mp"),
            P(("groups", "hosts"), "mp"),
        ),
        check_vma=False,
    )
```

profile of v0, /device:TPU:0, one launch (start us, length us, event | category | flops | bytes accessed | tf_op | source)
XLA Modules:
  0.0 238.8 jit_solution(13844421475531033518)
XLA Ops:
  3.2 6.3 %all-to-all-start.1 = ((bf16[4,8,1]{1,2,0:T(2,128)(2,1)}), bf16[4,8,1]{1,2,0:T(2,128)(2,1)S(1)}, u32[]{:S(2)}, u32[]{:S(2)}) async-start(bf16[4,8,1]{1,2,0:T(2,128)(2,1)} %reshape.598), calls=%async_computation.1 | async-start | bytes 4096 | tf_op jit(solution)/shard_map/all_to_all | solution.py:122
  15.3 1.7 fusion.14
  20.2 1.8 fusion.207
  23.4 5.1 %all-to-all-start.3 = ((bf16[4,8,4]{1,2,0:T(4,128)(2,1)}), bf16[4,8,4]{1,2,0:T(4,128)(2,1)S(1)}, u32[]{:S(2)}, u32[]{:S(2)}) async-start(bf16[4,8,4]{1,2,0:T(4,128)(2,1)} %copy.229), calls=%async_computation.3 | async-start | bytes 8192 | tf_op jit(solution)/shard_map/all_to_all | solution.py:172
  28.5 5.6 %all-to-all-done.3 = bf16[4,8,4]{1,2,0:T(4,128)(2,1)S(1)} async-done(((bf16[4,8,4]{1,2,0:T(4,128)(2,1)}), bf16[4,8,4]{1,2,0:T(4,128)(2,1)S(1)}, u32[]{:S(2)}, u32[]{:S(2)}) %all-to-all-start.3) | async-done | bytes 288 | tf_op jit(solution)/shard_map/all_to_all | solution.py:172
  34.1 3.2 %all-to-all-start.6 = ((bf16[4,8,4]{1,2,0:T(4,128)(2,1)}), bf16[4,8,4]{1,2,0:T(4,128)(2,1)S(1)}, u32[]{:S(2)}, u32[]{:S(2)}) async-start(bf16[4,8,4]{1,2,0:T(4,128)(2,1)} %copy.235), calls=%async_computation.6 | async-start | bytes 8192 | tf_op jit(solution)/shard_map/all_to_all | solution.py:172
  37.9 4.8 %all-to-all-done.6 = bf16[4,8,4]{1,2,0:T(4,128)(2,1)S(1)} async-done(((bf16[4,8,4]{1,2,0:T(4,128)(2,1)}), bf16[4,8,4]{1,2,0:T(4,128)(2,1)S(1)}, u32[]{:S(2)}, u32[]{:S(2)}) %all-to-all-start.6) | async-done | bytes 288 | tf_op jit(solution)/shard_map/all_to_all | solution.py:172
  42.7 3.2 %all-to-all-start.9 = ((bf16[4,8,4]{1,2,0:T(4,128)(2,1)}), bf16[4,8,4]{1,2,0:T(4,128)(2,1)S(1)}, u32[]{:S(2)}, u32[]{:S(2)}) async-start(bf16[4,8,4]{1,2,0:T(4,128)(2,1)} %copy.240), calls=%async_computation.9 | async-start | bytes 8192 | tf_op jit(solution)/shard_map/all_to_all | solution.py:172
  46.6 4.9 %all-to-all-done.9 = bf16[4,8,4]{1,2,0:T(4,128)(2,1)S(1)} async-done(((bf16[4,8,4]{1,2,0:T(4,128)(2,1)}), bf16[4,8,4]{1,2,0:T(4,128)(2,1)S(1)}, u32[]{:S(2)}, u32[]{:S(2)}) %all-to-all-start.9) | async-done | bytes 288 | tf_op jit(solution)/shard_map/all_to_all | solution.py:172
  51.5 3.3 %all-to-all-start = ((bf16[4,8,1024]{2,1,0:T(8,128)(2,1)}), bf16[4,8,1024]{2,1,0:T(8,128)(2,1)S(1)}, u32[]{:S(2)}, u32[]{:S(2)}) async-start(bf16[4,8,1024]{2,1,0:T(8,128)(2,1)} %fusion.14), calls=%async_computation | async-start | bytes 131072 | tf_op jit(solution)/shard_map/all_to_all | solution.py:121
  55.4 5.1 %all-to-all-done = bf16[4,8,1024]{2,1,0:T(8,128)(2,1)S(1)} async-done(((bf16[4,8,1024]{2,1,0:T(8,128)(2,1)}), bf16[4,8,1024]{2,1,0:T(8,128)(2,1)S(1)}, u32[]{:S(2)}, u32[]{:S(2)}) %all-to-all-start) | async-done | bytes 65568 | tf_op jit(solution)/shard_map/all_to_all | solution.py:121
  60.5 3.2 %all-to-all-start.12 = ((bf16[4,8,4]{1,2,0:T(4,128)(2,1)}), bf16[4,8,4]{1,2,0:T(4,128)(2,1)S(1)}, u32[]{:S(2)}, u32[]{:S(2)}) async-start(bf16[4,8,4]{1,2,0:T(4,128)(2,1)} %copy.245), calls=%async_computation.12 | async-start | bytes 8192 | tf_op jit(solution)/shard_map/all_to_all | solution.py:172
  63.9 10.4 %psum.7 = bf16[4,8,128]{2,1,0:T(8,128)(2,1)S(1)} all-reduce(f32[4,8,128]{2,1,0:T(8,128)S(1)} %convolution_multiply_fusion.8), channel_id=1, replica_groups=mesh['groups'=2,'hosts'=4,'mp'=4] {'mp'}, use_global_device_ids=true, to_apply=%region_2.3 | all-reduce | flops 4096 | bytes 24576 | tf_op jit(solution)/shard_map/psum | solution.py:127
  77.2 4.8 %all-to-all-start.2 = ((bf16[4,8,2048]{2,1,0:T(8,128)(2,1)}), bf16[4,8,2048]{2,1,0:T(8,128)(2,1)S(1)}, u32[]{:S(2)}, u32[]{:S(2)}) async-start(bf16[4,8,2048]{2,1,0:T(8,128)(2,1)} %fusion.52), calls=%async_computation.2 | async-start | bytes 262144 | tf_op jit(solution)/shard_map/all_to_all | solution.py:144
  82.6 5.3 %all-to-all-done.2 = bf16[4,8,2048]{2,1,0:T(8,128)(2,1)S(1)} async-done(((bf16[4,8,2048]{2,1,0:T(8,128)(2,1)}), bf16[4,8,2048]{2,1,0:T(8,128)(2,1)S(1)}, u32[]{:S(2)}, u32[]{:S(2)}) %all-to-all-start.2) | async-done | bytes 131104 | tf_op jit(solution)/shard_map/all_to_all | solution.py:144
  89.4 3.3 %all-to-all-start.13 = ((bf16[4,8,1024]{2,1,0:T(8,128)(2,1)}), bf16[4,8,1024]{2,1,0:T(8,128)(2,1)S(1)}, u32[]{:S(2)}, u32[]{:S(2)}) async-start(bf16[4,8,1024]{2,1,0:T(8,128)(2,1)} %fusion.18), calls=%async_computation.13 | async-start | bytes 131072 | tf_op jit(solution)/shard_map/all_to_all | solution.py:171
  92.7 1.6 broadcast_select_fusion
  94.4 1.8 fusion.24
  99.1 5.0 %all-to-all-start.10 = ((bf16[4,8,1024]{2,1,0:T(8,128)(2,1)}), bf16[4,8,1024]{2,1,0:T(8,128)(2,1)S(1)}, u32[]{:S(2)}, u32[]{:S(2)}) async-start(bf16[4,8,1024]{2,1,0:T(8,128)(2,1)} %fusion.17), calls=%async_computation.10 | async-start | bytes 131072 | tf_op jit(solution)/shard_map/all_to_all | solution.py:171
  105.1 4.8 %all-to-all-done.10 = bf16[4,8,1024]{2,1,0:T(8,128)(2,1)S(1)} async-done(((bf16[4,8,1024]{2,1,0:T(8,128)(2,1)}), bf16[4,8,1024]{2,1,0:T(8,128)(2,1)S(1)}, u32[]{:S(2)}, u32[]{:S(2)}) %all-to-all-start.10) | async-done | bytes 65568 | tf_op jit(solution)/shard_map/all_to_all | solution.py:171
  109.9 3.3 %all-to-all-start.7 = ((bf16[4,8,1024]{2,1,0:T(8,128)(2,1)}), bf16[4,8,1024]{2,1,0:T(8,128)(2,1)S(1)}, u32[]{:S(2)}, u32[]{:S(2)}) async-start(bf16[4,8,1024]{2,1,0:T(8,128)(2,1)} %fusion.16), calls=%async_computation.7 | async-start | bytes 131072 | tf_op jit(solution)/shard_map/all_to_all | solution.py:171
  114.2 4.7 %all-to-all-done.7 = bf16[4,8,1024]{2,1,0:T(8,128)(2,1)S(1)} async-done(((bf16[4,8,1024]{2,1,0:T(8,128)(2,1)}), bf16[4,8,1024]{2,1,0:T(8,128)(2,1)S(1)}, u32[]{:S(2)}, u32[]{:S(2)}) %all-to-all-start.7) | async-done | bytes 65568 | tf_op jit(solution)/shard_map/all_to_all | solution.py:171
  118.9 3.3 %all-to-all-start.4 = ((bf16[4,8,1024]{2,1,0:T(8,128)(2,1)}), bf16[4,8,1024]{2,1,0:T(8,128)(2,1)S(1)}, u32[]{:S(2)}, u32[]{:S(2)}) async-start(bf16[4,8,1024]{2,1,0:T(8,128)(2,1)} %fusion.15), calls=%async_computation.4 | async-start | bytes 131072 | tf_op jit(solution)/shard_map/all_to_all | solution.py:171
  127.9 4.3 %all-to-all-start.20 = ((f32[4,8,8]{1,2,0:T(8,128)}), f32[4,8,8]{1,2,0:T(8,128)S(1)}, u32[]{:S(2)}, u32[]{:S(2)}) async-start(f32[4,8,8]{1,2,0:T(8,128)} %copy.265), calls=%async_computation.20 | async-start | bytes 32768 | tf_op jit(solution)/shard_map/all_to_all | solution.py:179
  133.4 1.3 copy.238
  134.7 3.1 %all-to-all-done.20 = f32[4,8,8]{1,2,0:T(8,128)S(1)} async-done(((f32[4,8,8]{1,2,0:T(8,128)}), f32[4,8,8]{1,2,0:T(8,128)S(1)}, u32[]{:S(2)}, u32[]{:S(2)}) %all-to-all-start.20) | async-done | bytes 1056 | tf_op jit(solution)/shard_map/all_to_all | solution.py:179
  137.9 3.3 %all-to-all-start.8 = ((f32[4,8,8]{1,2,0:T(8,128)}), f32[4,8,8]{1,2,0:T(8,128)S(1)}, u32[]{:S(2)}, u32[]{:S(2)}) async-start(f32[4,8,8]{1,2,0:T(8,128)} %copy.238), calls=%async_computation.8 | async-start | bytes 32768 | tf_op jit(solution)/shard_map/all_to_all | solution.py:178
  142.7 4.0 %all-to-all-done.8 = f32[4,8,8]{1,2,0:T(8,128)S(1)} async-done(((f32[4,8,8]{1,2,0:T(8,128)}), f32[4,8,8]{1,2,0:T(8,128)S(1)}, u32[]{:S(2)}, u32[]{:S(2)}) %all-to-all-start.8) | async-done | bytes 1056 | tf_op jit(solution)/shard_map/all_to_all | solution.py:178
  146.7 3.2 %all-to-all-start.21 = ((f32[4,8,8]{1,2,0:T(8,128)}), f32[4,8,8]{1,2,0:T(8,128)S(1)}, u32[]{:S(2)}, u32[]{:S(2)}) async-start(f32[4,8,8]{1,2,0:T(8,128)} %copy.267), calls=%async_computation.21 | async-start | bytes 32768 | tf_op jit(solution)/shard_map/all_to_all | solution.py:179
  151.7 3.9 %all-to-all-done.21 = f32[4,8,8]{1,2,0:T(8,128)S(1)} async-done(((f32[4,8,8]{1,2,0:T(8,128)}), f32[4,8,8]{1,2,0:T(8,128)S(1)}, u32[]{:S(2)}, u32[]{:S(2)}) %all-to-all-start.21) | async-done | bytes 1056 | tf_op jit(solution)/shard_map/all_to_all | solution.py:179
  155.5 3.3 %all-to-all-start.11 = ((f32[4,8,8]{1,2,0:T(8,128)}), f32[4,8,8]{1,2,0:T(8,128)S(1)}, u32[]{:S(2)}, u32[]{:S(2)}) async-start(f32[4,8,8]{1,2,0:T(8,128)} %copy.243), calls=%async_computation.11 | async-start | bytes 32768 | tf_op jit(solution)/shard_map/all_to_all | solution.py:178
  160.4 4.0 %all-to-all-done.11 = f32[4,8,8]{1,2,0:T(8,128)S(1)} async-done(((f32[4,8,8]{1,2,0:T(8,128)}), f32[4,8,8]{1,2,0:T(8,128)S(1)}, u32[]{:S(2)}, u32[]{:S(2)}) %all-to-all-start.11) | async-done | bytes 1056 | tf_op jit(solution)/shard_map/all_to_all | solution.py:178
  164.4 3.2 %all-to-all-start.22 = ((f32[4,8,8]{1,2,0:T(8,128)}), f32[4,8,8]{1,2,0:T(8,128)S(1)}, u32[]{:S(2)}, u32[]{:S(2)}) async-start(f32[4,8,8]{1,2,0:T(8,128)} %copy.269), calls=%async_computation.22 | async-start | bytes 32768 | tf_op jit(solution)/shard_map/all_to_all | solution.py:179
  169.4 3.8 %all-to-all-done.22 = f32[4,8,8]{1,2,0:T(8,128)S(1)} async-done(((f32[4,8,8]{1,2,0:T(8,128)}), f32[4,8,8]{1,2,0:T(8,128)S(1)}, u32[]{:S(2)}, u32[]{:S(2)}) %all-to-all-start.22) | async-done | bytes 1056 | tf_op jit(solution)/shard_map/all_to_all | solution.py:179
  173.2 3.2 %all-to-all-start.14 = ((f32[4,8,8]{1,2,0:T(8,128)}), f32[4,8,8]{1,2,0:T(8,128)S(1)}, u32[]{:S(2)}, u32[]{:S(2)}) async-start(f32[4,8,8]{1,2,0:T(8,128)} %copy.248), calls=%async_computation.14 | async-start | bytes 32768 | tf_op jit(solution)/shard_map/all_to_all | solution.py:178
  180.7 1.3 all-to-all-done.14
  182.0 3.7 %all-to-all-start.19 = ((f32[4,8,8]{1,2,0:T(8,128)}), f32[4,8,8]{1,2,0:T(8,128)S(1)}, u32[]{:S(2)}, u32[]{:S(2)}) async-start(f32[4,8,8]{1,2,0:T(8,128)} %copy.263), calls=%async_computation.19 | async-start | bytes 32768 | tf_op jit(solution)/shard_map/all_to_all | solution.py:179
  186.1 5.3 %all-to-all-done.19 = f32[4,8,8]{1,2,0:T(8,128)S(1)} async-done(((f32[4,8,8]{1,2,0:T(8,128)}), f32[4,8,8]{1,2,0:T(8,128)S(1)}, u32[]{:S(2)}, u32[]{:S(2)}) %all-to-all-start.19) | async-done | bytes 1056 | tf_op jit(solution)/shard_map/all_to_all | solution.py:179
  191.4 3.3 %all-to-all-start.5 = ((f32[4,8,8]{1,2,0:T(8,128)}), f32[4,8,8]{1,2,0:T(8,128)S(1)}, u32[]{:S(2)}, u32[]{:S(2)}) async-start(f32[4,8,8]{1,2,0:T(8,128)} %copy.233), calls=%async_computation.5 | async-start | bytes 32768 | tf_op jit(solution)/shard_map/all_to_all | solution.py:178
  195.3 4.9 %all-to-all-done.5 = f32[4,8,8]{1,2,0:T(8,128)S(1)} async-done(((f32[4,8,8]{1,2,0:T(8,128)}), f32[4,8,8]{1,2,0:T(8,128)S(1)}, u32[]{:S(2)}, u32[]{:S(2)}) %all-to-all-start.5) | async-done | bytes 1056 | tf_op jit(solution)/shard_map/all_to_all | solution.py:178
  200.2 3.3 %all-to-all-start.16 = ((f32[4,8,1024]{2,1,0:T(8,128)}), f32[4,8,1024]{2,1,0:T(8,128)S(1)}, u32[]{:S(2)}, u32[]{:S(2)}) async-start(f32[4,8,1024]{2,1,0:T(8,128)} %bitcast.311), calls=%async_computation.16 | async-start | bytes 262144 | tf_op jit(solution)/shard_map/all_to_all | solution.py:177
  204.9 4.5 %all-to-all-done.16 = f32[4,8,1024]{2,1,0:T(8,128)S(1)} async-done(((f32[4,8,1024]{2,1,0:T(8,128)}), f32[4,8,1024]{2,1,0:T(8,128)S(1)}, u32[]{:S(2)}, u32[]{:S(2)}) %all-to-all-start.16) | async-done | bytes 131104 | tf_op jit(solution)/shard_map/all_to_all | solution.py:177
  209.4 3.3 %all-to-all-start.17 = ((f32[4,8,1024]{2,1,0:T(8,128)}), f32[4,8,1024]{2,1,0:T(8,128)S(1)}, u32[]{:S(2)}, u32[]{:S(2)}) async-start(f32[4,8,1024]{2,1,0:T(8,128)} %bitcast.310), calls=%async_computation.17 | async-start | bytes 262144 | tf_op jit(solution)/shard_map/all_to_all | solution.py:177
  213.0 6.0 %all-to-all-done.17 = f32[4,8,1024]{2,1,0:T(8,128)S(1)} async-done(((f32[4,8,1024]{2,1,0:T(8,128)}), f32[4,8,1024]{2,1,0:T(8,128)S(1)}, u32[]{:S(2)}, u32[]{:S(2)}) %all-to-all-start.17) | async-done | bytes 131104 | tf_op jit(solution)/shard_map/all_to_all | solution.py:177
  219.0 3.6 %all-to-all-start.18 = ((f32[4,8,1024]{2,1,0:T(8,128)}), f32[4,8,1024]{2,1,0:T(8,128)S(1)}, u32[]{:S(2)}, u32[]{:S(2)}) async-start(f32[4,8,1024]{2,1,0:T(8,128)} %bitcast.309), calls=%async_computation.18 | async-start | bytes 262144 | tf_op jit(solution)/shard_map/all_to_all | solution.py:177
  222.9 5.7 %all-to-all-done.18 = f32[4,8,1024]{2,1,0:T(8,128)S(1)} async-done(((f32[4,8,1024]{2,1,0:T(8,128)}), f32[4,8,1024]{2,1,0:T(8,128)S(1)}, u32[]{:S(2)}, u32[]{:S(2)}) %all-to-all-start.18) | async-done | bytes 131104 | tf_op jit(solution)/shard_map/all_to_all | solution.py:177
  228.5 3.3 %all-to-all-start.15 = ((f32[4,8,1024]{2,1,0:T(8,128)}), f32[4,8,1024]{2,1,0:T(8,128)S(1)}, u32[]{:S(2)}, u32[]{:S(2)}) async-start(f32[4,8,1024]{2,1,0:T(8,128)} %bitcast.312), calls=%async_computation.15 | async-start | bytes 262144 | tf_op jit(solution)/shard_map/all_to_all | solution.py:177
  232.1 5.6 %all-to-all-done.15 = f32[4,8,1024]{2,1,0:T(8,128)S(1)} async-done(((f32[4,8,1024]{2,1,0:T(8,128)}), f32[4,8,1024]{2,1,0:T(8,128)S(1)}, u32[]{:S(2)}, u32[]{:S(2)}) %all-to-all-start.15) | async-done | bytes 131104 | tf_op jit(solution)/shard_map/all_to_all | solution.py:177
  (214 shorter events, 45.3 us)
Async XLA Ops:
  0.6 63.1 %copy-start = (bf16[1,1024,128]{2,1,0:T(8,128)(2,1)S(1)}, bf16[1,1024,128]{2,1,0:T(8,128)(2,1)}, u32[]{:S(2)}) copy-start(bf16[1,1024,128]{2,1,0:T(8,128)(2,1)} %param.17) | copy-start | bytes 786436
  1.4 91.3 %copy-start.21 = (pred[32]{0:T(512)(128)(4,1)}, pred[32]{0:T(512)(128)(4,1)S(1)}, u32[]{:S(2)}) copy-start(pred[32]{0:T(512)(128)(4,1)S(1)} %iota_compare_fusion.15) | copy-start | bytes 100
  3.2 20.2 %all-to-all-start.1 = ((bf16[4,8,1]{1,2,0:T(2,128)(2,1)}), bf16[4,8,1]{1,2,0:T(2,128)(2,1)S(1)}, u32[]{:S(2)}, u32[]{:S(2)}) async-start(bf16[4,8,1]{1,2,0:T(2,128)(2,1)} %reshape.598), calls=%async_computation.1 | async-start | bytes 4096 | tf_op jit(solution)/shard_map/all_to_all | solution.py:122
  11.0 77.5 %copy-start.23 = (pred[32]{0:T(512)(128)(4,1)}, pred[32]{0:T(512)(128)(4,1)S(1)}, u32[]{:S(2)}) copy-start(pred[32]{0:T(512)(128)(4,1)S(1)} %get-tuple-element.47) | copy-start | bytes 100
  11.1 87.1 %copy-start.25 = (pred[32]{0:T(512)(128)(4,1)}, pred[32]{0:T(512)(128)(4,1)S(1)}, u32[]{:S(2)}) copy-start(pred[32]{0:T(512)(128)(4,1)S(1)} %get-tuple-element.48) | copy-start | bytes 100
  11.1 93.1 %copy-start.27 = (pred[32]{0:T(512)(128)(4,1)}, pred[32]{0:T(512)(128)(4,1)S(1)}, u32[]{:S(2)}) copy-start(pred[32]{0:T(512)(128)(4,1)S(1)} %get-tuple-element.49) | copy-start | bytes 100
  11.1 102.1 %copy-start.29 = (pred[32]{0:T(512)(128)(4,1)}, pred[32]{0:T(512)(128)(4,1)S(1)}, u32[]{:S(2)}) copy-start(pred[32]{0:T(512)(128)(4,1)S(1)} %get-tuple-element.46) | copy-start | bytes 100
  11.2 102.0 %copy-start.38 = (s32[32]{0:T(128)}, s32[32]{0:T(128)S(1)}, u32[]{:S(2)}) copy-start(s32[32]{0:T(128)S(1)} %multiply_add_fusion.4) | copy-start | bytes 388
  11.3 86.9 %copy-start.34 = (s32[32]{0:T(128)}, s32[32]{0:T(128)S(1)}, u32[]{:S(2)}) copy-start(s32[32]{0:T(128)S(1)} %multiply_add_fusion.2) | copy-start | bytes 388
  11.4 92.8 %copy-start.36 = (s32[32]{0:T(128)}, s32[32]{0:T(128)S(1)}, u32[]{:S(2)}) copy-start(s32[32]{0:T(128)S(1)} %multiply_add_fusion.3) | copy-start | bytes 388
  11.5 77.0 %copy-start.32 = (s32[32]{0:T(128)}, s32[32]{0:T(128)S(1)}, u32[]{:S(2)}) copy-start(s32[32]{0:T(128)S(1)} %multiply_add_fusion.1) | copy-start | bytes 388
  23.4 64.8 %copy-start.9 = (bf16[32,1024]{1,0:T(8,128)(2,1)S(1)}, bf16[32,1024]{1,0:T(8,128)(2,1)}, u32[]{:S(2)}) copy-start(bf16[32,1024]{1,0:T(8,128)(2,1)} %param.14) | copy-start | bytes 196612
  23.4 10.7 %all-to-all-start.3 = ((bf16[4,8,4]{1,2,0:T(4,128)(2,1)}), bf16[4,8,4]{1,2,0:T(4,128)(2,1)S(1)}, u32[]{:S(2)}, u32[]{:S(2)}) async-start(bf16[4,8,4]{1,2,0:T(4,128)(2,1)} %copy.229), calls=%async_computation.3 | async-start | bytes 8192 | tf_op jit(solution)/shard_map/all_to_all | solution.py:172
  34.1 8.6 %all-to-all-start.6 = ((bf16[4,8,4]{1,2,0:T(4,128)(2,1)}), bf16[4,8,4]{1,2,0:T(4,128)(2,1)S(1)}, u32[]{:S(2)}, u32[]{:S(2)}) async-start(bf16[4,8,4]{1,2,0:T(4,128)(2,1)} %copy.235), calls=%async_computation.6 | async-start | bytes 8192 | tf_op jit(solution)/shard_map/all_to_all | solution.py:172
  42.7 8.8 %all-to-all-start.9 = ((bf16[4,8,4]{1,2,0:T(4,128)(2,1)}), bf16[4,8,4]{1,2,0:T(4,128)(2,1)S(1)}, u32[]{:S(2)}, u32[]{:S(2)}) async-start(bf16[4,8,4]{1,2,0:T(4,128)(2,1)} %copy.240), calls=%async_computation.9 | async-start | bytes 8192 | tf_op jit(solution)/shard_map/all_to_all | solution.py:172
  51.5 9.0 %all-to-all-start = ((bf16[4,8,1024]{2,1,0:T(8,128)(2,1)}), bf16[4,8,1024]{2,1,0:T(8,128)(2,1)S(1)}, u32[]{:S(2)}, u32[]{:S(2)}) async-start(bf16[4,8,1024]{2,1,0:T(8,128)(2,1)} %fusion.14), calls=%async_computation | async-start | bytes 131072 | tf_op jit(solution)/shard_map/all_to_all | solution.py:121
  60.5 16.7 %all-to-all-start.12 = ((bf16[4,8,4]{1,2,0:T(4,128)(2,1)}), bf16[4,8,4]{1,2,0:T(4,128)(2,1)S(1)}, u32[]{:S(2)}, u32[]{:S(2)}) async-start(bf16[4,8,4]{1,2,0:T(4,128)(2,1)} %copy.245), calls=%async_computation.12 | async-start | bytes 8192 | tf_op jit(solution)/shard_map/all_to_all | solution.py:172
  77.2 10.7 %all-to-all-start.2 = ((bf16[4,8,2048]{2,1,0:T(8,128)(2,1)}), bf16[4,8,2048]{2,1,0:T(8,128)(2,1)S(1)}, u32[]{:S(2)}, u32[]{:S(2)}) async-start(bf16[4,8,2048]{2,1,0:T(8,128)(2,1)} %fusion.52), calls=%async_computation.2 | async-start | bytes 262144 | tf_op jit(solution)/shard_map/all_to_all | solution.py:144
  89.4 9.7 %all-to-all-start.13 = ((bf16[4,8,1024]{2,1,0:T(8,128)(2,1)}), bf16[4,8,1024]{2,1,0:T(8,128)(2,1)S(1)}, u32[]{:S(2)}, u32[]{:S(2)}) async-start(bf16[4,8,1024]{2,1,0:T(8,128)(2,1)} %fusion.18), calls=%async_computation.13 | async-start | bytes 131072 | tf_op jit(solution)/shard_map/all_to_all | solution.py:171
  99.1 10.8 %all-to-all-start.10 = ((bf16[4,8,1024]{2,1,0:T(8,128)(2,1)}), bf16[4,8,1024]{2,1,0:T(8,128)(2,1)S(1)}, u32[]{:S(2)}, u32[]{:S(2)}) async-start(bf16[4,8,1024]{2,1,0:T(8,128)(2,1)} %fusion.17), calls=%async_computation.10 | async-start | bytes 131072 | tf_op jit(solution)/shard_map/all_to_all | solution.py:171
  109.9 9.0 %all-to-all-start.7 = ((bf16[4,8,1024]{2,1,0:T(8,128)(2,1)}), bf16[4,8,1024]{2,1,0:T(8,128)(2,1)S(1)}, u32[]{:S(2)}, u32[]{:S(2)}) async-start(bf16[4,8,1024]{2,1,0:T(8,128)(2,1)} %fusion.16), calls=%async_computation.7 | async-start | bytes 131072 | tf_op jit(solution)/shard_map/all_to_all | solution.py:171
  118.9 9.0 %all-to-all-start.4 = ((bf16[4,8,1024]{2,1,0:T(8,128)(2,1)}), bf16[4,8,1024]{2,1,0:T(8,128)(2,1)S(1)}, u32[]{:S(2)}, u32[]{:S(2)}) async-start(bf16[4,8,1024]{2,1,0:T(8,128)(2,1)} %fusion.15), calls=%async_computation.4 | async-start | bytes 131072 | tf_op jit(solution)/shard_map/all_to_all | solution.py:171
  127.9 10.0 %all-to-all-start.20 = ((f32[4,8,8]{1,2,0:T(8,128)}), f32[4,8,8]{1,2,0:T(8,128)S(1)}, u32[]{:S(2)}, u32[]{:S(2)}) async-start(f32[4,8,8]{1,2,0:T(8,128)} %copy.265), calls=%async_computation.20 | async-start | bytes 32768 | tf_op jit(solution)/shard_map/all_to_all | solution.py:179
  137.9 8.8 %all-to-all-start.8 = ((f32[4,8,8]{1,2,0:T(8,128)}), f32[4,8,8]{1,2,0:T(8,128)S(1)}, u32[]{:S(2)}, u32[]{:S(2)}) async-start(f32[4,8,8]{1,2,0:T(8,128)} %copy.238), calls=%async_computation.8 | async-start | bytes 32768 | tf_op jit(solution)/shard_map/all_to_all | solution.py:178
  146.7 8.8 %all-to-all-start.21 = ((f32[4,8,8]{1,2,0:T(8,128)}), f32[4,8,8]{1,2,0:T(8,128)S(1)}, u32[]{:S(2)}, u32[]{:S(2)}) async-start(f32[4,8,8]{1,2,0:T(8,128)} %copy.267), calls=%async_computation.21 | async-start | bytes 32768 | tf_op jit(solution)/shard_map/all_to_all | solution.py:179
  151.0 27.6 %copy-start.8 = (f32[8,4,1,8,128]{4,3,2,1,0:T(8,128)S(1)}, f32[8,4,1,8,128]{4,3,2,1,0:T(8,128)}, u32[]{:S(2)}) copy-start(f32[8,4,1,8,128]{4,3,2,1,0:T(8,128)} %convolution_bitcast_fusion) | copy-start | bytes 393220
  151.0 28.2 %copy-start.7 = (f32[8,4,1,8,128]{4,3,2,1,0:T(8,128)S(1)}, f32[8,4,1,8,128]{4,3,2,1,0:T(8,128)}, u32[]{:S(2)}) copy-start(f32[8,4,1,8,128]{4,3,2,1,0:T(8,128)} %convolution_bitcast_fusion.1) | copy-start | bytes 393220
  151.0 28.9 %copy-start.6 = (f32[8,4,1,8,128]{4,3,2,1,0:T(8,128)S(1)}, f32[8,4,1,8,128]{4,3,2,1,0:T(8,128)}, u32[]{:S(2)}) copy-start(f32[8,4,1,8,128]{4,3,2,1,0:T(8,128)} %convolution_bitcast_fusion.2) | copy-start | bytes 393220
  155.5 8.8 %all-to-all-start.11 = ((f32[4,8,8]{1,2,0:T(8,128)}), f32[4,8,8]{1,2,0:T(8,128)S(1)}, u32[]{:S(2)}, u32[]{:S(2)}) async-start(f32[4,8,8]{1,2,0:T(8,128)} %copy.243), calls=%async_computation.11 | async-start | bytes 32768 | tf_op jit(solution)/shard_map/all_to_all | solution.py:178
  158.8 26.9 %copy-start.28 = (pred[32]{0:T(512)(128)(4,1)S(1)}, pred[32]{0:T(512)(128)(4,1)}, u32[]{:S(2)}) copy-start(pred[32]{0:T(512)(128)(4,1)} %copy-done.27) | copy-start | bytes 100
  159.8 34.9 %copy-start.26 = (pred[32]{0:T(512)(128)(4,1)S(1)}, pred[32]{0:T(512)(128)(4,1)}, u32[]{:S(2)}) copy-start(pred[32]{0:T(512)(128)(4,1)} %copy-done.25) | copy-start | bytes 100
  159.8 34.9 %copy-start.35 = (s32[32]{0:T(128)S(1)}, s32[32]{0:T(128)}, u32[]{:S(2)}) copy-start(s32[32]{0:T(128)} %copy-done.34) | copy-start | bytes 388
  164.4 8.8 %all-to-all-start.22 = ((f32[4,8,8]{1,2,0:T(8,128)}), f32[4,8,8]{1,2,0:T(8,128)S(1)}, u32[]{:S(2)}, u32[]{:S(2)}) async-start(f32[4,8,8]{1,2,0:T(8,128)} %copy.269), calls=%async_computation.22 | async-start | bytes 32768 | tf_op jit(solution)/shard_map/all_to_all | solution.py:179
  167.6 36.0 %copy-start.30 = (pred[32]{0:T(512)(128)(4,1)S(1)}, pred[32]{0:T(512)(128)(4,1)}, u32[]{:S(2)}) copy-start(pred[32]{0:T(512)(128)(4,1)} %copy-done.29) | copy-start | bytes 100
  167.6 36.0 %copy-start.39 = (s32[32]{0:T(128)S(1)}, s32[32]{0:T(128)}, u32[]{:S(2)}) copy-start(s32[32]{0:T(128)} %copy-done.38) | copy-start | bytes 388
  167.6 36.2 %copy-start.20 = (f32[32,8]{0,1:T(8,128)S(1)}, f32[32,8]{0,1:T(8,128)}, u32[]{:S(2)}) copy-start(f32[32,8]{0,1:T(8,128)} %copy-done.19) | copy-start | bytes 3076
  167.7 36.2 %copy-start.24 = (pred[32]{0:T(512)(128)(4,1)S(1)}, pred[32]{0:T(512)(128)(4,1)}, u32[]{:S(2)}) copy-start(pred[32]{0:T(512)(128)(4,1)} %copy-done.23) | copy-start | bytes 100
  167.7 36.2 %copy-start.33 = (s32[32]{0:T(128)S(1)}, s32[32]{0:T(128)}, u32[]{:S(2)}) copy-start(s32[32]{0:T(128)} %copy-done.32) | copy-start | bytes 388
  167.7 36.4 %copy-start.31 = (f32[32,8]{0,1:T(8,128)S(1)}, f32[32,8]{0,1:T(8,128)}, u32[]{:S(2)}) copy-start(f32[32,8]{0,1:T(8,128)} %get-tuple-element.27) | copy-start | bytes 3076
  173.2 8.8 %all-to-all-start.14 = ((f32[4,8,8]{1,2,0:T(8,128)}), f32[4,8,8]{1,2,0:T(8,128)S(1)}, u32[]{:S(2)}, u32[]{:S(2)}) async-start(f32[4,8,8]{1,2,0:T(8,128)} %copy.248), calls=%async_computation.14 | async-start | bytes 32768 | tf_op jit(solution)/shard_map/all_to_all | solution.py:178
  178.6 59.1 %copy-start.40 = (f32[32,8,1,128]{3,2,1,0:T(1,128)S(1)}, f32[32,8,1,128]{3,2,1,0:T(1,128)}, u32[]{:S(2)}) copy-start(f32[32,8,1,128]{3,2,1,0:T(1,128)} %fusion.28) | copy-start | bytes 393220
  180.6 57.4 %copy-start.22 = (pred[32]{0:T(512)(128)(4,1)S(1)}, pred[32]{0:T(512)(128)(4,1)}, u32[]{:S(2)}) copy-start(pred[32]{0:T(512)(128)(4,1)} %copy-done.21) | copy-start | bytes 100
  182.0 9.3 %all-to-all-start.19 = ((f32[4,8,8]{1,2,0:T(8,128)}), f32[4,8,8]{1,2,0:T(8,128)S(1)}, u32[]{:S(2)}, u32[]{:S(2)}) async-start(f32[4,8,8]{1,2,0:T(8,128)} %copy.263), calls=%async_computation.19 | async-start | bytes 32768 | tf_op jit(solution)/shard_map/all_to_all | solution.py:179
  191.4 8.8 %all-to-all-start.5 = ((f32[4,8,8]{1,2,0:T(8,128)}), f32[4,8,8]{1,2,0:T(8,128)S(1)}, u32[]{:S(2)}, u32[]{:S(2)}) async-start(f32[4,8,8]{1,2,0:T(8,128)} %copy.233), calls=%async_computation.5 | async-start | bytes 32768 | tf_op jit(solution)/shard_map/all_to_all | solution.py:178
  200.2 9.2 %all-to-all-start.16 = ((f32[4,8,1024]{2,1,0:T(8,128)}), f32[4,8,1024]{2,1,0:T(8,128)S(1)}, u32[]{:S(2)}, u32[]{:S(2)}) async-start(f32[4,8,1024]{2,1,0:T(8,128)} %bitcast.311), calls=%async_computation.16 | async-start | bytes 262144 | tf_op jit(solution)/shard_map/all_to_all | solution.py:177
  209.4 9.6 %all-to-all-start.17 = ((f32[4,8,1024]{2,1,0:T(8,128)}), f32[4,8,1024]{2,1,0:T(8,128)S(1)}, u32[]{:S(2)}, u32[]{:S(2)}) async-start(f32[4,8,1024]{2,1,0:T(8,128)} %bitcast.310), calls=%async_computation.17 | async-start | bytes 262144 | tf_op jit(solution)/shard_map/all_to_all | solution.py:177
  219.0 9.5 %all-to-all-start.18 = ((f32[4,8,1024]{2,1,0:T(8,128)}), f32[4,8,1024]{2,1,0:T(8,128)S(1)}, u32[]{:S(2)}, u32[]{:S(2)}) async-start(f32[4,8,1024]{2,1,0:T(8,128)} %bitcast.309), calls=%async_computation.18 | async-start | bytes 262144 | tf_op jit(solution)/shard_map/all_to_all | solution.py:177
  228.5 9.2 %all-to-all-start.15 = ((f32[4,8,1024]{2,1,0:T(8,128)}), f32[4,8,1024]{2,1,0:T(8,128)S(1)}, u32[]{:S(2)}, u32[]{:S(2)}) async-start(f32[4,8,1024]{2,1,0:T(8,128)} %bitcast.312), calls=%async_computation.15 | async-start | bytes 262144 | tf_op jit(solution)/shard_map/all_to_all | solution.py:177
  (16 other events, 227.1 us)
where the time goes:
time: 241 us; the launch traced here: 239 us
  waiting for transfers between devices  88.2 us (37%)
  starting transfers between devices  85.2 us (35%)
  matrix products  21.9 us (9%)
  local copies, waits for them, and re-layouts  18 us (7%)
  other arithmetic  12.8 us (5%)
  blocking collectives  10.4 us (4%)
    all_to_all x4, waiting for transfers between devices, body(): lax.all_to_all(answer_mixed_rows, 'hosts', split_axis=0, concat_axis=0, t...  21.8 us
    all_to_all x4, waiting for transfers between devices, body(): lax.all_to_all(answer_totals, 'hosts', split_axis=0, concat_axis=0, tiled...  16.1 us
    all_to_all x4, waiting for transfers between devices, body(): lax.all_to_all(request[3], 'hosts', split_axis=0, concat_axis=0, tiled=True)  15.3 us
    all_to_all x4, starting transfers between devices, body(): lax.all_to_all(request[2], 'hosts', split_axis=0, concat_axis=0, tiled=True)  14.9 us
    all_to_all x4, starting transfers between devices, body(): lax.all_to_all(request[3], 'hosts', split_axis=0, concat_axis=0, tiled=True)  14.8 us
    all_to_all x4, starting transfers between devices, body(): lax.all_to_all(answer_totals, 'hosts', split_axis=0, concat_axis=0, tiled...  14.5 us
    all_to_all x4, waiting for transfers between devices, body(): lax.all_to_all(answer_top_score, 'hosts', split_axis=0, concat_axis=0, ti...  14.2 us
    all_to_all x4, starting transfers between devices, body(): lax.all_to_all(answer_mixed_rows, 'hosts', split_axis=0, concat_axis=0, t...  13.5 us
  transfers between devices with their start and end apart: 23, of which 20 were waited for; matrix products, arithmetic and copies ran while one was open for 20% of the time, Pallas kernels for 0%

commit v1 on v0

--- a/solution.py
+++ b/solution.py
@@ -1,6 +1,8 @@
 import jax
 import jax.numpy as jnp
 from jax import lax
+from jax.experimental import pallas as pl
+from jax.experimental.pallas import tpu as pltpu
 from jax.sharding import PartitionSpec as P
 
 HEAD_SIZE = 128
@@ -81,7 +83,7 @@
     return (mixed_rows.reshape(queries.shape), top_score, totals)
 
 
-def body(
+def routed_body(
     hidden,
     base_query_projection,
     base_key_projection,
@@ -241,6 +243,487 @@
     )
 
 
+SMEM = pl.BlockSpec(memory_space=pltpu.SMEM)
+VMEM = pl.BlockSpec(memory_space=pltpu.VMEM)
+F32 = jnp.float32
+BF16 = jnp.bfloat16
+
+
+def shape_of(*dims, kind=BF16):
+    return jax.ShapeDtypeStruct(dims, kind)
+
+
+def host_offset(value, total):
+    return jnp.where(value < 0, value + total, value)
+
+
+def place_attempts(me, total, capacity, theorem_ref, live_ref, owner_ref, taken_ref):
+    for r in range(total):
+        taken_ref[r] = 0
+    live = live_ref[0]
+    slots = []
+    for a in range(theorem_ref.shape[0]):
+        r = host_offset(owner_ref[theorem_ref[a]] - me, total)
+        k = taken_ref[r]
+        fits = jnp.logical_and(a < live, k < capacity)
+        taken_ref[r] = jnp.where(fits, k + 1, k)
+        slots.append(jnp.where(fits, r * capacity + k, -1))
+    return slots
+
+
+def pack_matrix(slots, slot_total):
+    lanes = lax.broadcasted_iota(jnp.int32, (8, 128), 1)
+    rows = lax.broadcasted_iota(jnp.int32, (8, 128), 0)
+    wanted = jnp.full((8, 128), -1, jnp.int32)
+    for a, slot in enumerate(slots):
+        wanted = jnp.where(lanes == a, slot, wanted)
+    pieces = [
+        jnp.where(wanted == rows + base, 1.0, 0.0).astype(F32) for base in range(0, slot_total, 8)
+    ]
+    return jnp.concatenate(pieces, axis=0)[:, : len(slots)].astype(BF16)
+
+
+def unpack_matrix(slots, slot_total):
+    lanes = lax.broadcasted_iota(jnp.int32, (8, 128), 1)
+    rows = lax.broadcasted_iota(jnp.int32, (8, 128), 0)
+    pieces = []
+    for base in range(0, len(slots), 8):
+        wanted = jnp.full((8, 128), -1, jnp.int32)
+        for k in range(8):
+            wanted = jnp.where(rows == k, slots[base + k], wanted)
+        pieces.append(jnp.where(wanted == lanes, 1.0, 0.0).astype(F32))
+    return jnp.concatenate(pieces, axis=0)[:, :slot_total].astype(BF16)
+
+
+def dot(left, right):
+    return jnp.dot(left, right, preferred_element_type=F32)
+
+
+def turn(values, cosine, sine):
+    parts = []
+    for base in range(0, values.shape[1], HEAD_SIZE):
+        piece = values[:, base : base + HEAD_SIZE]
+        parts.append(piece * cosine + pltpu.roll(piece, HEAD_SIZE // 2, 1) * sine)
+    return jnp.concatenate(parts, axis=1)
+
+
+def send_kernel(total, capacity, theorem_ref, live_ref, owner_ref, hidden_ref, query_ref, *rest):
+    outs, taken_ref = rest[:total], rest[total]
+    me = lax.axis_index("hosts")
+    slots = place_attempts(me, total, capacity, theorem_ref, live_ref, owner_ref, taken_ref)
+    router = pack_matrix(slots, total * capacity)
+    packed_hidden = dot(router, hidden_ref[...])
+    packed_query = dot(router, query_ref[...])
+    for r in range(total):
+        rows = slice(r * capacity, (r + 1) * capacity)
+        outs[r][...] = jnp.concatenate([packed_hidden[rows], packed_query[rows]], axis=0).astype(
+            BF16
+        )
+
+
+def table_kernel(
+    total,
+    capacity,
+    theorem_ref,
+    live_ref,
+    owner_ref,
+    prefix_ref,
+    count_ref,
+    key_ref,
+    value_ref,
+    cosine_ref,
+    sine_ref,
+    key_rows_ref,
+    new_key_ref,
+    packed_value_ref,
+    unpack_ref,
+    meta_ref,
+    taken_ref,
+):
+    me = lax.axis_index("hosts")
+    slot_total = total * capacity
+    theorems = owner_ref.shape[0]
+    blocks = theorems * PBLK // total
+    slots = place_attempts(me, total, capacity, theorem_ref, live_ref, owner_ref, taken_ref)
+    for s in range(slot_total):
+        meta_ref[s] = 0
+    for a, slot in enumerate(slots):
+        meta_ref[jnp.where(slot < 0, meta_ref.shape[0] - 1, slot)] = a
+    source_base, valid_base, place_base = slot_total, slot_total + blocks, slot_total + 2 * blocks
+    spare = meta_ref.shape[0] - 1
+    for t in range(theorems):
+        owner = owner_ref[t]
+        r = host_offset(owner - me, total)
+        for j in range(PBLK):
+            block = prefix_ref[t, j]
+            holder = block // blocks
+            inner = block - holder * blocks
+            mine = holder == me
+            meta_ref[jnp.where(mine, source_base + inner, spare)] = host_offset(me - owner, total)
+            meta_ref[jnp.where(mine, valid_base + inner, spare)] = jnp.where(j < count_ref[t], 1, 0)
+            meta_ref[place_base + r * PBLK + j] = host_offset(me - holder, total) * blocks + inner
+    router = pack_matrix(slots, slot_total)
+    back = unpack_matrix(slots, slot_total)
+    unpack_ref[...] = back
+    packed_value_ref[...] = dot(router, value_ref[...]).astype(BF16)
+    packed_key = dot(router, key_ref[...])
+    turned = []
+    for r in range(total):
+        turned.append(
+            turn(
+                packed_key[r * capacity : (r + 1) * capacity],
+                cosine_ref[r : r + 1, :],
+                sine_ref[r : r + 1, :],
+            )
+        )
+    new_key = jnp.concatenate(turned, axis=0).astype(BF16)
+    new_key_ref[...] = new_key
+    key_rows_ref[...] = dot(back, new_key).astype(BF16)
+
+
+def rank_kernel(total, capacity, *refs):
+    rows, factors_ref, out_ref = refs[:total], refs[total], refs[total + 1]
+    stacked = jnp.concatenate([ref[...] for ref in rows], axis=0)
+    product = dot(stacked, factors_ref[...])
+    out_ref[...] = jnp.concatenate(
+        [product[2 * capacity * s : 2 * capacity * s + capacity] for s in range(total)], axis=0
+    )
+
+
+def query_kernel(total, capacity, sums, *refs):
+    rows = refs[:total]
+    partials = refs[total : total + sums]
+    factors_ref, cosine_ref, sine_ref = refs[total + sums : total + sums + 3]
+    outs = refs[total + sums + 3 :]
+    slot_total = total * capacity
+    level = [ref[...] for ref in partials]
+    while len(level) > 1:
+        level = [level[i] + level[i + 1] for i in range(0, len(level), 2)]
+    rank = level[0].astype(BF16).astype(F32)
+    lanes = lax.broadcasted_iota(jnp.int32, rank.shape, 1)
+    split = jnp.concatenate(
+        [jnp.where(lanes < ADAPTER_RANK, rank, 0.0), jnp.where(lanes < ADAPTER_RANK, 0.0, rank)],
+        axis=0,
+    ).astype(BF16)
+    correction = (dot(split, factors_ref[...]) * ADAPTER_SCALE).astype(BF16).astype(F32)
+    base = jnp.concatenate([ref[...].astype(F32)[capacity:] for ref in rows], axis=0)
+    query = turn(base + correction[:slot_total], cosine_ref[0:1, :], sine_ref[0:1, :])
+    for s in range(total):
+        back = (total - s) % total
+        first = slot_total + back * capacity
+        outs[s][...] = jnp.concatenate(
+            [query, correction[first : first + capacity]], axis=0
+        ).astype(BF16)
+
+
+def prefix_kernel(total, capacity, meta_ref, cache_ref, *refs):
+    received, outs = refs[:total], refs[total : 2 * total]
+    queries_ref, mixed_ref = refs[2 * total :]
+    slot_total = total * capacity
+    blocks, _, tokens, width = cache_ref.shape
+    heads = width // HEAD_SIZE
+    for s in range(total):
+        queries_ref[s * slot_total : (s + 1) * slot_total, :] = received[s][0:slot_total, :]
+    lanes = lax.broadcasted_iota(jnp.int32, (slot_total, HEAD_SIZE), 1)
+    for b in range(blocks):
+        source = meta_ref[slot_total + b]
+        valid = meta_ref[slot_total + blocks + b]
+        query = queries_ref[pl.ds(pl.multiple_of(source * slot_total, slot_total), slot_total), :]
+        stats = jnp.zeros((slot_total, HEAD_SIZE), F32)
+        for h in range(heads):
+            part = slice(h * HEAD_SIZE, (h + 1) * HEAD_SIZE)
+            scores = lax.dot_general(
+                query[:, part],
+                cache_ref[b, 0, :, part],
+                (((1,), (1,)), ((), ())),
+                preferred_element_type=F32,
+            ) * HEAD_SIZE ** (-0.5)
+            peak = jnp.max(scores, axis=1, keepdims=True)
+            weights = jnp.exp(scores - peak)
+            sums = jnp.sum(weights, axis=1, keepdims=True)
+            stats = jnp.where(lanes == h, peak, stats)
+            stats = jnp.where(lanes == heads + h, sums, stats)
+            mixed_ref[b, :, part] = dot(weights.astype(BF16), cache_ref[b, 1, :, part])
+        stats = jnp.where(jnp.logical_and(valid == 0, lanes < heads), NEG_FILL, stats)
+        high = stats.astype(BF16).astype(F32)
+        rest = stats - high
+        middle = rest.astype(BF16).astype(F32)
+        low = rest - middle
+        mixed_ref[b, :, width:] = (
+            high + pltpu.roll(middle, 2 * heads, 1) + pltpu.roll(low, 4 * heads, 1)
+        )
+        for s in range(total):
+            group = host_offset(host_offset(-source, total) - s, total)
+            outs[s][b] = mixed_ref[
+                b, pl.ds(pl.multiple_of(group * capacity, capacity), capacity), :
+            ].astype(BF16)
+
+
+def head_ones(width, transposed):
+    heads = width // HEAD_SIZE
+    if transposed:
+        rows = lax.broadcasted_iota(jnp.int32, (HEAD_SIZE, width), 0)
+        features = lax.broadcasted_iota(jnp.int32, (HEAD_SIZE, width), 1)
+    else:
+        rows = lax.broadcasted_iota(jnp.int32, (width, HEAD_SIZE), 1)
+        features = lax.broadcasted_iota(jnp.int32, (width, HEAD_SIZE), 0)
+    inside = jnp.logical_and(features >= rows * HEAD_SIZE, features < (rows + 1) * HEAD_SIZE)
+    return jnp.where(inside, 1.0, 0.0).astype(BF16)
+
+
+def head_sums(products, ones):
+    high = products.astype(BF16)
+    low = (products - high.astype(F32)).astype(BF16)
+    return dot(high, ones) + dot(low, ones)
+
+
+def own_kernel(total, capacity, meta_ref, cache_ref, new_key_ref, packed_value_ref, unpack_ref, *refs):
+    received = refs[:total]
+    value_rows_ref, mixed_ref, peak_ref, sums_ref, product_ref = refs[total:]
+    slot_total = total * capacity
+    suffix = cache_ref.shape[2]
+    width = cache_ref.shape[3]
+    ones = head_ones(width, False)
+    spread = head_ones(width, True)
+    queries, corrections = [], []
+    for r in range(total):
+        full = received[(total - r) % total][...].astype(F32)
+        queries.append(full[r * capacity : (r + 1) * capacity])
+        corrections.append(full[slot_total : slot_total + capacity])
+    query = jnp.concatenate(queries, axis=0)
+    new_value = (packed_value_ref[...].astype(F32) + jnp.concatenate(corrections, axis=0)).astype(
+        BF16
+    )
+    value_rows_ref[...] = dot(unpack_ref[...], new_value).astype(BF16)
+    for s in range(slot_total):
+        keys = cache_ref[meta_ref[s], 0].astype(F32)
+        product_ref[s * suffix : (s + 1) * suffix, :] = keys * query[s : s + 1, :]
+    scale = HEAD_SIZE ** (-0.5)
+    scores = (head_sums(product_ref[...], ones) * scale).reshape(slot_total, suffix, HEAD_SIZE)
+    new_scores = head_sums(new_key_ref[...].astype(F32) * query, ones) * scale
+    peak = jnp.maximum(jnp.max(scores, axis=1), new_scores)
+    weights = jnp.exp(scores - peak[:, None, :])
+    new_weights = jnp.exp(new_scores - peak)
+    peak_ref[...] = peak
+    sums_ref[...] = jnp.sum(weights, axis=1) + new_weights
+    product_ref[...] = dot(weights.reshape(slot_total * suffix, HEAD_SIZE).astype(BF16), spread)
+    mixed_ref[...] = dot(new_weights.astype(BF16), spread) * new_value.astype(F32)
+    for s in range(slot_total):
+        values = cache_ref[meta_ref[s], 1].astype(F32)
+        mixed_ref[s : s + 1, :] += jnp.sum(
+            product_ref[s * suffix : (s + 1) * suffix, :] * values, axis=0, keepdims=True
+        )
+
+
+def combine_kernel(total, capacity, meta_ref, unpack_ref, mixed_ref, peak_ref, sums_ref, *refs):
+    received, out_ref, parts_ref = refs[:total], refs[total], refs[total + 1]
+    slot_total = total * capacity
+    blocks = received[0].shape[0]
+    width = mixed_ref.shape[1]
+    heads = width // HEAD_SIZE
+    for s in range(total):
+        parts_ref[s * blocks : (s + 1) * blocks] = received[s][...]
+    results = []
+    for r in range(total):
+        rows = slice(r * capacity, (r + 1) * capacity)
+        overall = peak_ref[rows, :]
+        pieces = []
+        for j in range(PBLK):
+            place = meta_ref[slot_total + 2 * blocks + r * PBLK + j]
+            coded = parts_ref[place, :, width:].astype(F32)
+            stats = (
+                coded
+                + pltpu.roll(coded, HEAD_SIZE - 2 * heads, 1)
+                + pltpu.roll(coded, HEAD_SIZE - 4 * heads, 1)
+            )
+            pieces.append((place, stats, pltpu.roll(stats, HEAD_SIZE - heads, 1)))
+            overall = jnp.maximum(overall, stats)
+        own_factor = jnp.exp(peak_ref[rows, :] - overall)
+        denominator = sums_ref[rows, :] * own_factor
+        factors = []
+        for place, top, sums in pieces:
+            factor = jnp.exp(top - overall)
+            factors.append(factor)
+            denominator = denominator + sums * factor
+        columns = []
+        for h in range(heads):
+            part = slice(h * HEAD_SIZE, (h + 1) * HEAD_SIZE)
+            numerator = mixed_ref[rows, part] * own_factor[:, h : h + 1]
+            for (place, _, _), factor in zip(pieces, factors):
+                numerator = numerator + parts_ref[place, :, part].astype(F32) * factor[:, h : h + 1]
+            columns.append(numerator / denominator[:, h : h + 1])
+        results.append(jnp.concatenate(columns, axis=1))
+    attended = jnp.concatenate(results, axis=0).astype(BF16)
+    out_ref[...] = dot(unpack_ref[...], attended).astype(BF16)
+
+
+def exchange(arrays):
+    total = len(arrays)
+    received = [arrays[0]]
+    for s in range(1, total):
+        ring = [(i, (i + s) % total) for i in range(total)]
+        received.append(lax.ppermute(arrays[s], "hosts", ring))
+    return received
+
+
+def direct_body(
+    hidden,
+    base_query_projection,
+    base_key_projection,
+    base_value_projection,
+    adapter_input_factors,
+    adapter_output_factors,
+    statement_prefix_cache,
+    generated_token_cache,
+    attempt_theorem_index,
+    host_live_count,
+    adapter_pool_row,
+    prefix_pool_row,
+    prefix_block_count,
+):
+    total = lax.axis_size("hosts")
+    shares = lax.axis_size("mp")
+    attempts, width = hidden.shape
+    capacity = attempts // total
+    slot_total = total * capacity
+    blocks = statement_prefix_cache.shape[0]
+    suffix = generated_token_cache.shape[2]
+    input_factors = adapter_input_factors[0]
+    output_factors = adapter_output_factors.reshape(2 * ADAPTER_RANK, width)
+    taken = pltpu.SMEM((total,), jnp.int32)
+
+    sent = pl.pallas_call(
+        lambda *refs: send_kernel(total, capacity, *refs),
+        out_shape=[shape_of(2 * capacity, width)] * total,
+        in_specs=[SMEM] * 3 + [VMEM] * 2,
+        out_specs=[VMEM] * total,
+        scratch_shapes=[taken],
+        name="send_rows",
+    )(attempt_theorem_index, host_live_count, adapter_pool_row, hidden, base_query_projection)
+    rows = exchange(sent)
+
+    me = lax.axis_index("hosts")
+    owners = (me + jnp.arange(total, dtype=jnp.int32)) % total
+    counts = jnp.sum(
+        jnp.where(
+            owners[:, None] == adapter_pool_row[None, :], prefix_block_count[None, :], 0
+        ),
+        axis=1,
+    )
+    position = (BLK * counts + suffix).astype(F32)
+    frequency = ROPE_BASE ** (
+        -(jnp.arange(HEAD_SIZE // 2, dtype=F32) * (2.0 / HEAD_SIZE))
+    )
+    angles = position[:, None] * frequency
+    cosine = jnp.cos(angles)
+    sine = jnp.sin(angles)
+    cosine = jnp.concatenate([cosine, cosine], axis=1)
+    sine = jnp.concatenate([-sine, sine], axis=1)
+
+    key_rows, new_key, packed_value, unpack, meta = pl.pallas_call(
+        lambda *refs: table_kernel(total, capacity, *refs),
+        out_shape=[
+            shape_of(attempts, width),
+            shape_of(slot_total, width),
+            shape_of(slot_total, width),
+            shape_of(attempts, slot_total),
+            shape_of(slot_total + 2 * blocks + total * PBLK + 1, kind=jnp.int32),
+        ],
+        in_specs=[SMEM] * 5 + [VMEM] * 4,
+        out_specs=[VMEM] * 4 + [SMEM],
+        scratch_shapes=[taken],
+        name="slot_tables",
+    )(
+        attempt_theorem_index,
+        host_live_count,
+        adapter_pool_row,
+        prefix_pool_row,
+        prefix_block_count,
+        base_key_projection,
+        base_value_projection,
+        cosine,
+        sine,
+    )
+
+    partial = pl.pallas_call(
+        lambda *refs: rank_kernel(total, capacity, *refs),
+        out_shape=shape_of(slot_total, 2 * ADAPTER_RANK, kind=F32),
+        in_specs=[VMEM] * (total + 1),
+        out_specs=VMEM,
+        name="rank_rows",
+    )(*rows, input_factors)
+    partials = [partial]
+    for s in range(1, shares):
+        partials.append(lax.ppermute(partial, "mp", [(i, i ^ s) for i in range(shares)]))
+
+    answers = pl.pallas_call(
+        lambda *refs: query_kernel(total, capacity, shares, *refs),
+        out_shape=[shape_of(slot_total + capacity, width)] * total,
+        in_specs=[VMEM] * (total + shares + 3),
+        out_specs=[VMEM] * total,
+        name="query_rows",
+    )(*rows, *partials, output_factors, cosine, sine)
+    queries = exchange(answers)
+
+    replies = pl.pallas_call(
+        lambda *refs: prefix_kernel(total, capacity, *refs),
+        out_shape=[shape_of(blocks, capacity, width + HEAD_SIZE)] * total,
+        in_specs=[SMEM] + [VMEM] * (total + 1),
+        out_specs=[VMEM] * total,
+        scratch_shapes=[
+            pltpu.VMEM((total * slot_total, width), BF16),
+            pltpu.VMEM((blocks, slot_total, width + HEAD_SIZE), F32),
+        ],
+        name="prefix_attention",
+    )(meta, statement_prefix_cache, *queries)
+    partial_rows = exchange(replies)
+
+    value_rows, mixed, peak, sums = pl.pallas_call(
+        lambda *refs: own_kernel(total, capacity, *refs),
+        out_shape=[
+            shape_of(attempts, width),
+            shape_of(slot_total, width, kind=F32),
+            shape_of(slot_total, HEAD_SIZE, kind=F32),
+            shape_of(slot_total, HEAD_SIZE, kind=F32),
+        ],
+        in_specs=[SMEM] + [VMEM] * (total + 4),
+        out_specs=[VMEM] * 4,
+        scratch_shapes=[pltpu.VMEM((slot_total * suffix, width), F32)],
+        name="own_attention",
+    )(meta, generated_token_cache, new_key, packed_value, unpack, *queries)
+
+    attended = pl.pallas_call(
+        lambda *refs: combine_kernel(total, capacity, *refs),
+        out_shape=shape_of(attempts, width),
+        in_specs=[SMEM] + [VMEM] * (total + 4),
+        out_specs=VMEM,
+        scratch_shapes=[pltpu.VMEM((total * blocks, capacity, width + HEAD_SIZE), BF16)],
+        name="combine",
+    )(meta, unpack, mixed, peak, sums, *partial_rows)
+    return attended, key_rows, value_rows
+
+
+def body(*arguments):
+    total = lax.axis_size("hosts")
+    shares = lax.axis_size("mp")
+    attempts, width = arguments[0].shape
+    theorems = arguments[10].shape[0]
+    blocks = arguments[6].shape[0]
+    suffix = arguments[7].shape[2]
+    direct = (
+        total <= 8
+        and shares & (shares - 1) == 0
+        and arguments[4].shape[0] == 1
+        and theorems == total
+        and blocks * total == theorems * PBLK
+        and attempts == 8 * total
+        and 2 * total * 8 <= 128
+        and suffix == 8
+        and 6 * (width // HEAD_SIZE) <= HEAD_SIZE
+    )
+    return direct_body(*arguments) if direct else routed_body(*arguments)
+
+
 def solution(mesh):
     placed = (
         P(("groups", "hosts"), "mp"),

time: 241 us -> 55.9 us (0.23)
  waiting for transfers between devices: 88.2 us -> 9.01 us
  starting transfers between devices: 85.2 us -> 17.2 us
  Pallas kernels: 0 us -> 23.9 us
  matrix products: 21.9 us -> 0 us
  local copies, waits for them, and re-layouts: 18 us -> 2.52 us
  other arithmetic: 12.8 us -> 1.66 us
  blocking collectives: 10.4 us -> 0 us
    all_to_all x23 -> x0, waiting for transfers between devices: 88.2 us -> none  [the longest x4 21.8 us: body(): lax.all_to_all(answer_mixed_rows, 'hosts', split_axis=0, concat_axis=0, t...]
    all_to_all x23 -> x0, starting transfers between devices: 85.2 us -> none  [the longest x4 14.9 us: body(): lax.all_to_all(request[2], 'hosts', split_axis=0, concat_axis=0, tiled=True)]
    pallas_call x0 -> x7, Pallas kernels: none -> 23.9 us  [the longest x1 10.2 us: direct_body(): pl.pallas_call(lambda *refs: prefix_kernel(total, capacity, *refs), out_s...]
    dot_general x36 -> x0, matrix products: 21.9 us -> none  [the longest x10 6.59 us: pack_rows(): jnp.dot(router, payload, preferred_element_type=jnp.float32)]
    ppermute x0 -> x12, starting transfers between devices: none -> 17.2 us  [the longest x9 15.3 us: exchange(): received.append(lax.ppermute(arrays[s], 'hosts', ring))]
    psum x1 -> x0, blocking collectives: 10.4 us -> none  [body(): rank_rows = lax.psum(partial_rank, 'mp').astype(jnp.bfloat16)]
    ppermute x0 -> x12, waiting for transfers between devices: none -> 9.01 us  [the longest x9 7.58 us: exchange(): received.append(lax.ppermute(arrays[s], 'hosts', ring))]
    reshape x21 -> x0, local copies, waits for them, and re-layouts: 6.78 us -> none  [the longest x8 2.76 us: body(): pack_rows(router, block_pick).reshape(host_total, capacity, local_blocks)]
  transfers between devices with their start and end apart: 23 -> 12, of which waited for: 20 -> 7; matrix products, arithmetic and copies ran while one was open for 20% -> 3% of each run, Pallas kernels for 0% -> 10%
where the time goes in v1:
time: 55.9 us; the launch traced here: 55.6 us
  Pallas kernels  23.9 us (43%)
  starting transfers between devices  17.2 us (31%)
  waiting for transfers between devices  9.01 us (16%)
  local copies, waits for them, and re-layouts  2.52 us (5%)
  other arithmetic  1.66 us (3%)
  between operations  1.35 us (2%)
    ppermute x9, starting transfers between devices, exchange(): received.append(lax.ppermute(arrays[s], 'hosts', ring))  15.3 us
    pallas_call x1, Pallas kernels, direct_body(): pl.pallas_call(lambda *refs: prefix_kernel(total, capacity, *refs), out_s...  10.2 us
    ppermute x9, waiting for transfers between devices, exchange(): received.append(lax.ppermute(arrays[s], 'hosts', ring))  7.58 us
    pallas_call x1, Pallas kernels, direct_body(): pl.pallas_call(lambda *refs: own_kernel(total, capacity, *refs), out_shap...  3.31 us
    unnamed x24, local copies, waits for them, and re-layouts  2.52 us
    pallas_call x1, Pallas kernels, direct_body(): pl.pallas_call(lambda *refs: combine_kernel(total, capacity, *refs), out_...  2.46 us
    pallas_call x1, Pallas kernels, direct_body(): pl.pallas_call(lambda *refs: table_kernel(total, capacity, *refs), out_sh...  2.14 us
    pallas_call x1, Pallas kernels, direct_body(): pl.pallas_call(lambda *refs: query_kernel(total, capacity, shares, *refs)...  2.07 us
  transfers between devices with their start and end apart: 12, of which 7 were waited for; matrix products, arithmetic and copies ran while one was open for 3% of the time, Pallas kernels for 10%

profile of v1, /device:TPU:0, one launch (start us, length us, event | category | flops | bytes accessed | tf_op | source)
XLA Modules:
  0.0 55.6 jit_solution(8236608263553587054)
XLA Ops:
  1.3 1.9 %send_rows.1 = (bf16[16,1024]{1,0:T(8,128)(2,1)}, bf16[16,1024]{1,0:T(8,128)(2,1)}, bf16[16,1024]{1,0:T(8,128)(2,1)}, bf16[16,1024]{1,0:T(8,128)(2,1)}) custom-call(s32[32]{0:T(128)} %refs_0_.3, s32[1]{0:T(128)S(6)} %copy.16.refs_1_, s32[4]{0:T(128)} %refs_2_.3, bf16[32,1024]{1,0:T(8,128)(2,1)} %refs_3_.3, bf16[32,1024]{1,0:T(8,128)(2,1)} %refs_4_.3), custom_call_target="tpu_custom_call" | custom-call | tf_op jit(solution)/shard_map/send_rows/pallas_call | solution.py:595
  3.2 3.1 %collective-permute-start = (bf16[16,1024]{1,0:T(8,128)(2,1)}, bf16[16,1024]{1,0:T(8,128)(2,1)S(1)}, u32[]{:S(2)}, u32[]{:S(2)}) collective-permute-start(bf16[16,1024]{1,0:T(8,128)(2,1)} %get-tuple-element.29), channel_id=1, source_target_pairs={{0,4},{4,8},{8,12},{12,0},{1,5},{5,9},{9,13},{13,1},{2,6},{6,10},{... | collective-permute-start | bytes 98312 | tf_op jit(solution)/shard_map/ppermute | solution.py:565
  6.3 2.6 %collective-permute-start.1 = (bf16[16,1024]{1,0:T(8,128)(2,1)}, bf16[16,1024]{1,0:T(8,128)(2,1)S(1)}, u32[]{:S(2)}, u32[]{:S(2)}) collective-permute-start(bf16[16,1024]{1,0:T(8,128)(2,1)} %get-tuple-element.30), channel_id=1, source_target_pairs={{0,8},{4,12},{8,0},{12,4},{1,9},{5,13},{9,1},{13,5},{2,10},{6,14},... | collective-permute-start | bytes 98312 | tf_op jit(solution)/shard_map/ppermute | solution.py:565
  8.8 1.3 %collective-permute-start.2 = (bf16[16,1024]{1,0:T(8,128)(2,1)}, bf16[16,1024]{1,0:T(8,128)(2,1)S(1)}, u32[]{:S(2)}, u32[]{:S(2)}) collective-permute-start(bf16[16,1024]{1,0:T(8,128)(2,1)} %get-tuple-element.31), channel_id=1, source_target_pairs={{0,12},{4,0},{8,4},{12,8},{1,13},{5,1},{9,5},{13,9},{2,14},{6,2},{... | collective-permute-start | bytes 98312 | tf_op jit(solution)/shard_map/ppermute | solution.py:565
  10.2 0.9 %select_reduce_fusion = s32[4]{0:T(128)S(1)} fusion(s32[4]{0:T(128)} %refs_4_.2, s32[4]{0:T(128)} %refs_2_.3, s32[4]{0:T(128)S(1)} %and_select_fusion), kind=kLoop, calls=%fused_computation.6 | loop fusion | flops 44 | bytes 64 | tf_op jit(solution)/shard_map/reduce_sum | solution.py:607
  11.1 0.1 fusion.1
  11.2 0.0 collective-permute-done.refs_1_
  11.2 0.0 copy-start.3
  11.2 0.4 collective-permute-done.1.refs_2_
  11.6 1.3 %collective-permute-done.2.refs_3_ = bf16[16,1024]{1,0:T(8,128)(2,1)S(1)} collective-permute-done((bf16[16,1024]{1,0:T(8,128)(2,1)}, bf16[16,1024]{1,0:T(8,128)(2,1)S(1)}, u32[]{:S(2)}, u32[]{:S(2)}) %collective-permute-start.2) | collective-permute-done | bytes 32800 | tf_op jit(solution)/shard_map/ppermute | solution.py:565
  13.0 0.0 copy-done.3
  13.0 0.0 copy-done.4
  13.0 0.6 %copy-done.5 = bf16[16,1024]{1,0:T(8,128)(2,1)} copy-done((bf16[16,1024]{1,0:T(8,128)(2,1)}, bf16[16,1024]{1,0:T(8,128)(2,1)S(1)}, u32[]{:S(2)}) %copy-start.5) | copy-done | bytes 32792
  13.6 1.8 %rank_rows.1.refs_4_ = f32[32,128]{1,0:T(8,128)} custom-call(bf16[16,1024]{1,0:T(8,128)(2,1)} %get-tuple-element.28.refs_0_, bf16[16,1024]{1,0:T(8,128)(2,1)} %copy-done.3, bf16[16,1024]{1,0:T(8,128)(2,1)} %copy-done.4, bf16[16,1024]{1,0:T(8,128)(2,1)} %copy-done.5, bf16[1024,128]{1,0:T(8,128)(2,1)} %bitcast.3), custom_call_target="tpu_custom_call" | custom-call | tf_op jit(solution)/shard_map/rank_rows/pallas_call | solution.py:648
  15.4 0.0 collective-permute-start.5
  15.4 1.5 %collective-permute-start.4 = (f32[32,128]{1,0:T(8,128)}, f32[32,128]{1,0:T(8,128)S(1)}, u32[]{:S(2)}, u32[]{:S(2)}) collective-permute-start(f32[32,128]{1,0:T(8,128)} %rank_rows.1.refs_4_), channel_id=1, source_target_pairs={{0,2},{1,3},{2,0},{3,1},{4,6},{5,7},{6,4},{7,5},{8,10},{9,11},{10,... | collective-permute-start | bytes 49160 | tf_op jit(solution)/shard_map/ppermute | solution.py:657
  16.9 0.4 collective-permute-start.3
  17.2 0.7 %pad_maximum_fusion = (f32[4,128]{1,0:T(4,128)}, f32[4,128]{1,0:T(4,128)}) fusion(f32[4,64]{1,0:T(4,128)S(1)} %get-tuple-element.47, f32[4,64]{1,0:T(4,128)S(1)} %get-tuple-element.46, f32[4,64]{1,0:T(4,128)S(1)} %get-tuple-element.45), kind=kLoop, calls=%fused_computation.4 | loop fusion | flops 1024 | bytes 7168 | tf_op jit(solution)/shard_map/concatenate | solution.py:620
  17.9 1.0 %collective-permute-done.5.refs_7_ = f32[32,128]{1,0:T(8,128)S(1)} collective-permute-done((f32[32,128]{1,0:T(8,128)}, f32[32,128]{1,0:T(8,128)S(1)}, u32[]{:S(2)}, u32[]{:S(2)}) %collective-permute-start.5) | collective-permute-done | bytes 16416 | tf_op jit(solution)/shard_map/ppermute | solution.py:657
  18.9 0.4 collective-permute-done.4.refs_6_
  19.3 0.0 collective-permute-done.3.refs_5_
  19.3 0.1 copy-done.9
  19.5 0.4 copy-done.10
  19.9 0.0 copy-done.11
  19.9 2.1 %query_rows.1 = (bf16[40,1024]{1,0:T(8,128)(2,1)}, bf16[40,1024]{1,0:T(8,128)(2,1)}, bf16[40,1024]{1,0:T(8,128)(2,1)}, bf16[40,1024]{1,0:T(8,128)(2,1)}) custom-call(bf16[16,1024]{1,0:T(8,128)(2,1)} %get-tuple-element.28.refs_0_, bf16[16,1024]{1,0:T(8,128)(2,1)} %copy-done.3, bf16[16,1024]{1,0:T(8,128)(2,1)} %copy-done.4, bf16[16,1024]{1,0:T(8,128)(2,1)} %copy-done.5, ...), custom_call_target="tpu_custom_call" | custom-call | tf_op jit(solution)/shard_map/query_rows/pallas_call | solution.py:659
  22.0 0.2 collective-permute-start.6
  22.2 3.5 %collective-permute-start.7 = (bf16[40,1024]{1,0:T(8,128)(2,1)}, bf16[40,1024]{1,0:T(8,128)(2,1)S(1)}, u32[]{:S(2)}, u32[]{:S(2)}) collective-permute-start(bf16[40,1024]{1,0:T(8,128)(2,1)} %get-tuple-element.34), channel_id=1, source_target_pairs={{0,8},{4,12},{8,0},{12,4},{1,9},{5,13},{9,1},{13,5},{2,10},{6,14},... | collective-permute-start | bytes 245768 | tf_op jit(solution)/shard_map/ppermute | solution.py:565
  25.7 0.1 collective-permute-start.8
  25.9 2.1 %slot_tables.1 = (bf16[32,1024]{1,0:T(8,128)(2,1)}, bf16[32,1024]{1,0:T(8,128)(2,1)}, bf16[32,1024]{1,0:T(8,128)(2,1)}, bf16[32,32]{1,0:T(8,128)(2,1)}, s32[57]{0:T(128)}) custom-call(s32[32]{0:T(128)} %refs_0_.3, s32[1]{0:T(128)S(6)} %copy.16.refs_1_, s32[4]{0:T(128)} %refs_2_.3, s32[4,4]{1,0:T(4,128)} %refs_3_.2, s32[4]{0:T(128)} %refs_4_.2, ...), custom_call_target="tpu_custom_call" | custom-call | tf_op jit(solution)/shard_map/slot_tables/pallas_call | solution.py:623
  28.0 1.4 %collective-permute-done.6.refs_6_.refs_3_ = bf16[40,1024]{1,0:T(8,128)(2,1)S(1)} collective-permute-done((bf16[40,1024]{1,0:T(8,128)(2,1)}, bf16[40,1024]{1,0:T(8,128)(2,1)S(1)}, u32[]{:S(2)}, u32[]{:S(2)}) %collective-permute-start.6) | collective-permute-done | bytes 81952 | tf_op jit(solution)/shard_map/ppermute | solution.py:565
  29.4 3.0 %collective-permute-done.7.refs_7_.refs_4_ = bf16[40,1024]{1,0:T(8,128)(2,1)S(1)} collective-permute-done((bf16[40,1024]{1,0:T(8,128)(2,1)}, bf16[40,1024]{1,0:T(8,128)(2,1)S(1)}, u32[]{:S(2)}, u32[]{:S(2)}) %collective-permute-start.7) | collective-permute-done | bytes 81952 | tf_op jit(solution)/shard_map/ppermute | solution.py:565
  32.4 0.0 collective-permute-done.8.refs_8_.refs_5_
  32.4 0.0 copy-done
  32.4 0.6 %copy-done.1 = bf16[40,1024]{1,0:T(8,128)(2,1)} copy-done((bf16[40,1024]{1,0:T(8,128)(2,1)}, bf16[40,1024]{1,0:T(8,128)(2,1)S(1)}, u32[]{:S(2)}) %copy-start.1) | copy-done | bytes 81944
  33.1 0.0 copy-done.2
  33.1 10.2 %prefix_attention.1 = (bf16[4,8,1152]{2,1,0:T(8,128)(2,1)}, bf16[4,8,1152]{2,1,0:T(8,128)(2,1)}, bf16[4,8,1152]{2,1,0:T(8,128)(2,1)}, bf16[4,8,1152]{2,1,0:T(8,128)(2,1)}) custom-call(s32[57]{0:T(128)} %get-tuple-element.24.refs_0_, bf16[4,2,128,1024]{3,2,1,0:T(8,128)(2,1)} %refs_1_.5, bf16[40,1024]{1,0:T(8,128)(2,1)} %get-tuple-element.32.refs_5_.refs_2_, ...), custom_call_target="tpu_custom_call" | custom-call | tf_op jit(solution)/shard_map/prefix_attention/pallas_call | solution.py:668
  43.3 2.1 %collective-permute-start.9 = (bf16[4,8,1152]{2,1,0:T(8,128)(2,1)}, bf16[4,8,1152]{2,1,0:T(8,128)(2,1)S(1)}, u32[]{:S(2)}, u32[]{:S(2)}) collective-permute-start(bf16[4,8,1152]{2,1,0:T(8,128)(2,1)} %get-tuple-element.40), channel_id=1, source_target_pairs={{0,4},{4,8},{8,12},{12,0},{1,5},{5,9},{9,13},{13,1},{2,6},{6,10},{... | collective-permute-start | bytes 221192 | tf_op jit(solution)/shard_map/ppermute | solution.py:565
  45.3 1.0 %collective-permute-start.10 = (bf16[4,8,1152]{2,1,0:T(8,128)(2,1)}, bf16[4,8,1152]{2,1,0:T(8,128)(2,1)S(1)}, u32[]{:S(2)}, u32[]{:S(2)}) collective-permute-start(bf16[4,8,1152]{2,1,0:T(8,128)(2,1)} %get-tuple-element.41), channel_id=1, source_target_pairs={{0,8},{4,12},{8,0},{12,4},{1,9},{5,13},{9,1},{13,5},{2,10},{6,14},... | collective-permute-start | bytes 221192 | tf_op jit(solution)/shard_map/ppermute | solution.py:565
  46.4 1.4 %collective-permute-start.11 = (bf16[4,8,1152]{2,1,0:T(8,128)(2,1)}, bf16[4,8,1152]{2,1,0:T(8,128)(2,1)S(1)}, u32[]{:S(2)}, u32[]{:S(2)}) collective-permute-start(bf16[4,8,1152]{2,1,0:T(8,128)(2,1)} %get-tuple-element.42), channel_id=1, source_target_pairs={{0,12},{4,0},{8,4},{12,8},{1,13},{5,1},{9,5},{13,9},{2,14},{6,2},{... | collective-permute-start | bytes 221192 | tf_op jit(solution)/shard_map/ppermute | solution.py:565
  47.7 3.3 %own_attention.1 = (bf16[32,1024]{1,0:T(8,128)(2,1)}, f32[32,1024]{1,0:T(8,128)}, f32[32,128]{1,0:T(8,128)}, f32[32,128]{1,0:T(8,128)}) custom-call(s32[57]{0:T(128)} %get-tuple-element.24.refs_0_, bf16[32,2,8,1024]{3,2,1,0:T(8,128)(2,1)} %refs_1_.4, bf16[32,1024]{1,0:T(8,128)(2,1)} %get-tuple-element.26.refs_2_, ...), custom_call_target="tpu_custom_call" | custom-call | tf_op jit(solution)/shard_map/own_attention/pallas_call | solution.py:681
  51.0 0.0 collective-permute-done.9.refs_6_
  51.0 0.0 copy-start.6
  51.1 1.4 %collective-permute-done.10.refs_7_ = bf16[4,8,1152]{2,1,0:T(8,128)(2,1)S(1)} collective-permute-done((bf16[4,8,1152]{2,1,0:T(8,128)(2,1)}, bf16[4,8,1152]{2,1,0:T(8,128)(2,1)S(1)}, u32[]{:S(2)}, u32[]{:S(2)}) %collective-permute-start.10) | collective-permute-done | bytes 73760 | tf_op jit(solution)/shard_map/ppermute | solution.py:565
  52.5 0.0 collective-permute-done.11.refs_8_
  52.5 0.0 copy-done.6
  52.5 0.6 %copy-done.7 = bf16[4,8,1152]{2,1,0:T(8,128)(2,1)} copy-done((bf16[4,8,1152]{2,1,0:T(8,128)(2,1)}, bf16[4,8,1152]{2,1,0:T(8,128)(2,1)S(1)}, u32[]{:S(2)}) %copy-start.7) | copy-done | bytes 73752
  53.1 0.0 copy-done.8
  53.1 2.5 %combine.1 = bf16[32,1024]{1,0:T(8,128)(2,1)} custom-call(s32[57]{0:T(128)} %get-tuple-element.24.refs_0_, bf16[32,32]{1,0:T(8,128)(2,1)} %get-tuple-element.25.refs_4_.refs_1_, f32[32,1024]{1,0:T(8,128)} %get-tuple-element.36.refs_2_, f32[32,128]{1,0:T(8,128)} %get-tuple-element.37.refs_3_, f32[32,128]{1,0:T(8,128)} %get-tuple-element.38.refs_4_, ...), custom_call_target="tpu_custom_call" | custom-call | tf_op jit(solution)/shard_map/combine/pallas_call | solution.py:695
  (13 shorter events, 0.0 us)
Async XLA Ops:
  3.2 8.0 %collective-permute-start = (bf16[16,1024]{1,0:T(8,128)(2,1)}, bf16[16,1024]{1,0:T(8,128)(2,1)S(1)}, u32[]{:S(2)}, u32[]{:S(2)}) collective-permute-start(bf16[16,1024]{1,0:T(8,128)(2,1)} %get-tuple-element.29), channel_id=1, source_target_pairs={{0,4},{4,8},{8,12},{12,0},{1,5},{5,9},{9,13},{13,1},{2,6},{6,10},{... | collective-permute-start | bytes 98312 | tf_op jit(solution)/shard_map/ppermute | solution.py:565
  6.3 5.4 %collective-permute-start.1 = (bf16[16,1024]{1,0:T(8,128)(2,1)}, bf16[16,1024]{1,0:T(8,128)(2,1)S(1)}, u32[]{:S(2)}, u32[]{:S(2)}) collective-permute-start(bf16[16,1024]{1,0:T(8,128)(2,1)} %get-tuple-element.30), channel_id=1, source_target_pairs={{0,8},{4,12},{8,0},{12,4},{1,9},{5,13},{9,1},{13,5},{2,10},{6,14},... | collective-permute-start | bytes 98312 | tf_op jit(solution)/shard_map/ppermute | solution.py:565
  8.8 4.1 %collective-permute-start.2 = (bf16[16,1024]{1,0:T(8,128)(2,1)}, bf16[16,1024]{1,0:T(8,128)(2,1)S(1)}, u32[]{:S(2)}, u32[]{:S(2)}) collective-permute-start(bf16[16,1024]{1,0:T(8,128)(2,1)} %get-tuple-element.31), channel_id=1, source_target_pairs={{0,12},{4,0},{8,4},{12,8},{1,13},{5,1},{9,5},{13,9},{2,14},{6,2},{... | collective-permute-start | bytes 98312 | tf_op jit(solution)/shard_map/ppermute | solution.py:565
  11.2 1.8 %copy-start.3 = (bf16[16,1024]{1,0:T(8,128)(2,1)}, bf16[16,1024]{1,0:T(8,128)(2,1)S(1)}, u32[]{:S(2)}) copy-start(bf16[16,1024]{1,0:T(8,128)(2,1)S(1)} %collective-permute-done.refs_1_) | copy-start | bytes 98308
  11.6 1.4 %copy-start.4 = (bf16[16,1024]{1,0:T(8,128)(2,1)}, bf16[16,1024]{1,0:T(8,128)(2,1)S(1)}, u32[]{:S(2)}) copy-start(bf16[16,1024]{1,0:T(8,128)(2,1)S(1)} %collective-permute-done.1.refs_2_) | copy-start | bytes 98308
  13.0 0.6 %copy-start.5 = (bf16[16,1024]{1,0:T(8,128)(2,1)}, bf16[16,1024]{1,0:T(8,128)(2,1)S(1)}, u32[]{:S(2)}) copy-start(bf16[16,1024]{1,0:T(8,128)(2,1)S(1)} %collective-permute-done.2.refs_3_) | copy-start | bytes 98308
  15.4 3.5 %collective-permute-start.5 = (f32[32,128]{1,0:T(8,128)}, f32[32,128]{1,0:T(8,128)S(1)}, u32[]{:S(2)}, u32[]{:S(2)}) collective-permute-start(f32[32,128]{1,0:T(8,128)} %rank_rows.1.refs_4_), channel_id=1, source_target_pairs={{0,3},{1,2},{2,1},{3,0},{4,7},{5,6},{6,5},{7,4},{8,11},{9,10},{10,... | collective-permute-start | bytes 49160 | tf_op jit(solution)/shard_map/ppermute | solution.py:657
  15.4 3.9 %collective-permute-start.4 = (f32[32,128]{1,0:T(8,128)}, f32[32,128]{1,0:T(8,128)S(1)}, u32[]{:S(2)}, u32[]{:S(2)}) collective-permute-start(f32[32,128]{1,0:T(8,128)} %rank_rows.1.refs_4_), channel_id=1, source_target_pairs={{0,2},{1,3},{2,0},{3,1},{4,6},{5,7},{6,4},{7,5},{8,10},{9,11},{10,... | collective-permute-start | bytes 49160 | tf_op jit(solution)/shard_map/ppermute | solution.py:657
  16.9 2.5 %collective-permute-start.3 = (f32[32,128]{1,0:T(8,128)}, f32[32,128]{1,0:T(8,128)S(1)}, u32[]{:S(2)}, u32[]{:S(2)}) collective-permute-start(f32[32,128]{1,0:T(8,128)} %rank_rows.1.refs_4_), channel_id=1, source_target_pairs={{0,1},{1,0},{2,3},{3,2},{4,5},{5,4},{6,7},{7,6},{8,9},{9,8},{10,11... | collective-permute-start | bytes 49160 | tf_op jit(solution)/shard_map/ppermute | solution.py:657
  18.9 0.6 %copy-start.9 = (f32[32,128]{1,0:T(8,128)}, f32[32,128]{1,0:T(8,128)S(1)}, u32[]{:S(2)}) copy-start(f32[32,128]{1,0:T(8,128)S(1)} %collective-permute-done.5.refs_7_) | copy-start | bytes 49156
  19.3 0.6 %copy-start.10 = (f32[32,128]{1,0:T(8,128)}, f32[32,128]{1,0:T(8,128)S(1)}, u32[]{:S(2)}) copy-start(f32[32,128]{1,0:T(8,128)S(1)} %collective-permute-done.4.refs_6_) | copy-start | bytes 49156
  19.3 0.6 %copy-start.11 = (f32[32,128]{1,0:T(8,128)}, f32[32,128]{1,0:T(8,128)S(1)}, u32[]{:S(2)}) copy-start(f32[32,128]{1,0:T(8,128)S(1)} %collective-permute-done.3.refs_5_) | copy-start | bytes 49156
  22.0 7.4 %collective-permute-start.6 = (bf16[40,1024]{1,0:T(8,128)(2,1)}, bf16[40,1024]{1,0:T(8,128)(2,1)S(1)}, u32[]{:S(2)}, u32[]{:S(2)}) collective-permute-start(bf16[40,1024]{1,0:T(8,128)(2,1)} %get-tuple-element.33), channel_id=1, source_target_pairs={{0,4},{4,8},{8,12},{12,0},{1,5},{5,9},{9,13},{13,1},{2,6},{6,10},{... | collective-permute-start | bytes 245768 | tf_op jit(solution)/shard_map/ppermute | solution.py:565
  22.2 10.2 %collective-permute-start.7 = (bf16[40,1024]{1,0:T(8,128)(2,1)}, bf16[40,1024]{1,0:T(8,128)(2,1)S(1)}, u32[]{:S(2)}, u32[]{:S(2)}) collective-permute-start(bf16[40,1024]{1,0:T(8,128)(2,1)} %get-tuple-element.34), channel_id=1, source_target_pairs={{0,8},{4,12},{8,0},{12,4},{1,9},{5,13},{9,1},{13,5},{2,10},{6,14},... | collective-permute-start | bytes 245768 | tf_op jit(solution)/shard_map/ppermute | solution.py:565
  25.7 6.7 %collective-permute-start.8 = (bf16[40,1024]{1,0:T(8,128)(2,1)}, bf16[40,1024]{1,0:T(8,128)(2,1)S(1)}, u32[]{:S(2)}, u32[]{:S(2)}) collective-permute-start(bf16[40,1024]{1,0:T(8,128)(2,1)} %get-tuple-element.35), channel_id=1, source_target_pairs={{0,12},{4,0},{8,4},{12,8},{1,13},{5,1},{9,5},{13,9},{2,14},{6,2},{... | collective-permute-start | bytes 245768 | tf_op jit(solution)/shard_map/ppermute | solution.py:565
  29.4 3.0 %copy-start = (bf16[40,1024]{1,0:T(8,128)(2,1)}, bf16[40,1024]{1,0:T(8,128)(2,1)S(1)}, u32[]{:S(2)}) copy-start(bf16[40,1024]{1,0:T(8,128)(2,1)S(1)} %collective-permute-done.6.refs_6_.refs_3_) | copy-start | bytes 245764
  32.4 0.6 %copy-start.1 = (bf16[40,1024]{1,0:T(8,128)(2,1)}, bf16[40,1024]{1,0:T(8,128)(2,1)S(1)}, u32[]{:S(2)}) copy-start(bf16[40,1024]{1,0:T(8,128)(2,1)S(1)} %collective-permute-done.7.refs_7_.refs_4_) | copy-start | bytes 245764
  32.4 0.7 %copy-start.2 = (bf16[40,1024]{1,0:T(8,128)(2,1)}, bf16[40,1024]{1,0:T(8,128)(2,1)S(1)}, u32[]{:S(2)}) copy-start(bf16[40,1024]{1,0:T(8,128)(2,1)S(1)} %collective-permute-done.8.refs_8_.refs_5_) | copy-start | bytes 245764
  43.3 7.8 %collective-permute-start.9 = (bf16[4,8,1152]{2,1,0:T(8,128)(2,1)}, bf16[4,8,1152]{2,1,0:T(8,128)(2,1)S(1)}, u32[]{:S(2)}, u32[]{:S(2)}) collective-permute-start(bf16[4,8,1152]{2,1,0:T(8,128)(2,1)} %get-tuple-element.40), channel_id=1, source_target_pairs={{0,4},{4,8},{8,12},{12,0},{1,5},{5,9},{9,13},{13,1},{2,6},{6,10},{... | collective-permute-start | bytes 221192 | tf_op jit(solution)/shard_map/ppermute | solution.py:565
  45.3 7.1 %collective-permute-start.10 = (bf16[4,8,1152]{2,1,0:T(8,128)(2,1)}, bf16[4,8,1152]{2,1,0:T(8,128)(2,1)S(1)}, u32[]{:S(2)}, u32[]{:S(2)}) collective-permute-start(bf16[4,8,1152]{2,1,0:T(8,128)(2,1)} %get-tuple-element.41), channel_id=1, source_target_pairs={{0,8},{4,12},{8,0},{12,4},{1,9},{5,13},{9,1},{13,5},{2,10},{6,14},... | collective-permute-start | bytes 221192 | tf_op jit(solution)/shard_map/ppermute | solution.py:565
  46.4 6.1 %collective-permute-start.11 = (bf16[4,8,1152]{2,1,0:T(8,128)(2,1)}, bf16[4,8,1152]{2,1,0:T(8,128)(2,1)S(1)}, u32[]{:S(2)}, u32[]{:S(2)}) collective-permute-start(bf16[4,8,1152]{2,1,0:T(8,128)(2,1)} %get-tuple-element.42), channel_id=1, source_target_pairs={{0,12},{4,0},{8,4},{12,8},{1,13},{5,1},{9,5},{13,9},{2,14},{6,2},{... | collective-permute-start | bytes 221192 | tf_op jit(solution)/shard_map/ppermute | solution.py:565
  51.0 1.4 %copy-start.6 = (bf16[4,8,1152]{2,1,0:T(8,128)(2,1)}, bf16[4,8,1152]{2,1,0:T(8,128)(2,1)S(1)}, u32[]{:S(2)}) copy-start(bf16[4,8,1152]{2,1,0:T(8,128)(2,1)S(1)} %collective-permute-done.9.refs_6_) | copy-start | bytes 221188
  52.5 0.6 %copy-start.7 = (bf16[4,8,1152]{2,1,0:T(8,128)(2,1)}, bf16[4,8,1152]{2,1,0:T(8,128)(2,1)S(1)}, u32[]{:S(2)}) copy-start(bf16[4,8,1152]{2,1,0:T(8,128)(2,1)S(1)} %collective-permute-done.10.refs_7_) | copy-start | bytes 221188
  52.5 0.6 %copy-start.8 = (bf16[4,8,1152]{2,1,0:T(8,128)(2,1)}, bf16[4,8,1152]{2,1,0:T(8,128)(2,1)S(1)}, u32[]{:S(2)}) copy-start(bf16[4,8,1152]{2,1,0:T(8,128)(2,1)S(1)} %collective-permute-done.11.refs_8_) | copy-start | bytes 221188

commit v2 on v1

--- a/solution.py
+++ b/solution.py
@@ -245,6 +245,7 @@
 
 SMEM = pl.BlockSpec(memory_space=pltpu.SMEM)
 VMEM = pl.BlockSpec(memory_space=pltpu.VMEM)
+GRANT = pltpu.CompilerParams(vmem_limit_bytes=16 * 1024 * 1024)
 F32 = jnp.float32
 BF16 = jnp.bfloat16
 
@@ -599,6 +600,7 @@
         out_specs=[VMEM] * total,
         scratch_shapes=[taken],
         name="send_rows",
+        compiler_params=GRANT,
     )(attempt_theorem_index, host_live_count, adapter_pool_row, hidden, base_query_projection)
     rows = exchange(sent)
 
@@ -633,6 +635,7 @@
         out_specs=[VMEM] * 4 + [SMEM],
         scratch_shapes=[taken],
         name="slot_tables",
+        compiler_params=GRANT,
     )(
         attempt_theorem_index,
         host_live_count,
@@ -651,6 +654,7 @@
         in_specs=[VMEM] * (total + 1),
         out_specs=VMEM,
         name="rank_rows",
+        compiler_params=GRANT,
     )(*rows, input_factors)
     partials = [partial]
     for s in range(1, shares):
@@ -662,6 +666,7 @@
         in_specs=[VMEM] * (total + shares + 3),
         out_specs=[VMEM] * total,
         name="query_rows",
+        compiler_params=GRANT,
     )(*rows, *partials, output_factors, cosine, sine)
     queries = exchange(answers)
 
@@ -675,6 +680,7 @@
             pltpu.VMEM((blocks, slot_total, width + HEAD_SIZE), F32),
         ],
         name="prefix_attention",
+        compiler_params=GRANT,
     )(meta, statement_prefix_cache, *queries)
     partial_rows = exchange(replies)
 
@@ -690,6 +696,7 @@
         out_specs=[VMEM] * 4,
         scratch_shapes=[pltpu.VMEM((slot_total * suffix, width), F32)],
         name="own_attention",
+        compiler_params=GRANT,
     )(meta, generated_token_cache, new_key, packed_value, unpack, *queries)
 
     attended = pl.pallas_call(
@@ -699,6 +706,7 @@
         out_specs=VMEM,
         scratch_shapes=[pltpu.VMEM((total * blocks, capacity, width + HEAD_SIZE), BF16)],
         name="combine",
+        compiler_params=GRANT,
     )(meta, unpack, mixed, peak, sums, *partial_rows)
     return attended, key_rows, value_rows
 

time: 55.9 us -> 52.7 us (0.943)
  local copies, waits for them, and re-layouts: 2.52 us -> 10.8 us
  Pallas kernels: 23.9 us -> 15.7 us
  waiting for transfers between devices: 9.01 us -> 5.47 us
  starting transfers between devices: 17.2 us -> 17.8 us
  other arithmetic: 1.66 us -> 1.07 us
    unnamed x24 -> x28, local copies, waits for them, and re-layouts: 2.52 us -> 10.8 us
    ppermute x9, waiting for transfers between devices: 7.58 us -> 3.59 us  [exchange(): received.append(lax.ppermute(arrays[s], 'hosts', ring))]
    pallas_call x1, Pallas kernels: 10.2 us -> 8.29 us  [direct_body(): pl.pallas_call(lambda *refs: prefix_kernel(total, capacity, *refs), out_s...]
    pallas_call x1, Pallas kernels: 2.07 us -> 0.25 us  [direct_body(): pl.pallas_call(lambda *refs: query_kernel(total, capacity, shares, *refs)...]
    pallas_call x1, Pallas kernels: 1.8 us -> 0.18 us  [direct_body(): pl.pallas_call(lambda *refs: rank_kernel(total, capacity, *refs), out_sha...]
    pallas_call x1, Pallas kernels: 3.31 us -> 2.28 us  [direct_body(): pl.pallas_call(lambda *refs: own_kernel(total, capacity, *refs), out_shap...]
    pallas_call x1, Pallas kernels: 1.92 us -> 0.94 us  [direct_body(): pl.pallas_call(lambda *refs: send_kernel(total, capacity, *refs), out_sha...]
    concatenate x1, other arithmetic: 0.66 us -> 0.07 us  [direct_body(): cosine = jnp.concatenate([cosine, cosine], axis=1)]
  transfers between devices with their start and end apart: 12 -> 12, of which waited for: 7 -> 6; matrix products, arithmetic and copies ran while one was open for 3% -> 2% of each run, Pallas kernels for 10% -> 8%
where the time goes in v2:
time: 52.7 us; the launch traced here: 52.2 us
  starting transfers between devices  17.8 us (34%)
  Pallas kernels  15.7 us (30%)
  local copies, waits for them, and re-layouts  10.8 us (20%)
  waiting for transfers between devices  5.47 us (10%)
  between operations  1.47 us (3%)
  other arithmetic  1.07 us (2%)
    ppermute x9, starting transfers between devices, exchange(): received.append(lax.ppermute(arrays[s], 'hosts', ring))  15.8 us
    unnamed x28, local copies, waits for them, and re-layouts  10.8 us
    pallas_call x1, Pallas kernels, direct_body(): pl.pallas_call(lambda *refs: prefix_kernel(total, capacity, *refs), out_s...  8.29 us
    ppermute x9, waiting for transfers between devices, exchange(): received.append(lax.ppermute(arrays[s], 'hosts', ring))  3.59 us
    pallas_call x1, Pallas kernels, direct_body(): pl.pallas_call(lambda *refs: own_kernel(total, capacity, *refs), out_shap...  2.28 us
    ppermute x3, starting transfers between devices, direct_body(): lax.ppermute(partial, 'mp', [(i, i ^ s) for i in range(shares)])  1.92 us
    ppermute x3, waiting for transfers between devices, direct_body(): lax.ppermute(partial, 'mp', [(i, i ^ s) for i in range(shares)])  1.88 us
    pallas_call x1, Pallas kernels, direct_body(): pl.pallas_call(lambda *refs: combine_kernel(total, capacity, *refs), out_...  1.88 us
  transfers between devices with their start and end apart: 12, of which 6 were waited for; matrix products, arithmetic and copies ran while one was open for 2% of the time, Pallas kernels for 8%

profile of v2, /device:TPU:0, one launch (start us, length us, event | category | flops | bytes accessed | tf_op | source)
XLA Modules:
  0.0 52.2 jit_solution(9903418083603355861)
XLA Ops:
  0.6 0.0 copy-start.1
  1.4 0.8 %copy-done.4 = bf16[32,1024]{1,0:T(8,128)(2,1)S(1)} copy-done((bf16[32,1024]{1,0:T(8,128)(2,1)S(1)}, bf16[32,1024]{1,0:T(8,128)(2,1)}, u32[]{:S(2)}) %copy-start.4) | copy-done | bytes 65560
  2.2 0.8 %copy-done.5 = bf16[32,1024]{1,0:T(8,128)(2,1)S(1)} copy-done((bf16[32,1024]{1,0:T(8,128)(2,1)S(1)}, bf16[32,1024]{1,0:T(8,128)(2,1)}, u32[]{:S(2)}) %copy-start.5) | copy-done | bytes 65560
  3.1 0.7 %copy-done.8 = s32[4]{0:T(128)S(1)} copy-done((s32[4]{0:T(128)S(1)}, s32[4]{0:T(128)}, u32[]{:S(2)}) %copy-start.8) | copy-done | bytes 40
  3.7 0.7 %copy-done.11 = s32[32]{0:T(128)S(1)} copy-done((s32[32]{0:T(128)S(1)}, s32[32]{0:T(128)}, u32[]{:S(2)}) %copy-start.11) | copy-done | bytes 152
  4.4 0.9 %send_rows.1 = (bf16[16,1024]{1,0:T(8,128)(2,1)S(1)}, bf16[16,1024]{1,0:T(8,128)(2,1)S(1)}, bf16[16,1024]{1,0:T(8,128)(2,1)S(1)}, bf16[16,1024]{1,0:T(8,128)(2,1)S(1)}) custom-call(s32[32]{0:T(128)S(1)} %copy-done.11, s32[1]{0:T(128)S(6)} %copy.16.refs_1_, s32[4]{0:T(128)S(1)} %copy-done.8, bf16[32,1024]{1,0:T(8,128)(2,1)S(1)} %copy-done.4, ...), custom_call_target="tpu_custom_call" | custom-call | tf_op jit(solution)/shard_map/send_rows/pallas_call | solution.py:596
  5.3 3.1 %collective-permute-start = (bf16[16,1024]{1,0:T(8,128)(2,1)S(1)}, bf16[16,1024]{1,0:T(8,128)(2,1)S(1)}, u32[]{:S(2)}, u32[]{:S(2)}) collective-permute-start(bf16[16,1024]{1,0:T(8,128)(2,1)S(1)} %get-tuple-element.29), channel_id=1, source_target_pairs={{0,4},{4,8},{8,12},{12,0},{1,5},{5,9},{9,13},{13,1},{2,6},{6,10},{... | collective-permute-start | bytes 98312 | tf_op jit(solution)/shard_map/ppermute | solution.py:566
  8.4 2.6 %collective-permute-start.1 = (bf16[16,1024]{1,0:T(8,128)(2,1)S(1)}, bf16[16,1024]{1,0:T(8,128)(2,1)S(1)}, u32[]{:S(2)}, u32[]{:S(2)}) collective-permute-start(bf16[16,1024]{1,0:T(8,128)(2,1)S(1)} %get-tuple-element.30), channel_id=1, source_target_pairs={{0,8},{4,12},{8,0},{12,4},{1,9},{5,13},{9,1},{13,5},{2,10},{6,14},... | collective-permute-start | bytes 98312 | tf_op jit(solution)/shard_map/ppermute | solution.py:566
  11.0 1.3 %collective-permute-start.2 = (bf16[16,1024]{1,0:T(8,128)(2,1)S(1)}, bf16[16,1024]{1,0:T(8,128)(2,1)S(1)}, u32[]{:S(2)}, u32[]{:S(2)}) collective-permute-start(bf16[16,1024]{1,0:T(8,128)(2,1)S(1)} %get-tuple-element.31), channel_id=1, source_target_pairs={{0,12},{4,0},{8,4},{12,8},{1,13},{5,1},{9,5},{13,9},{2,14},{6,2},{... | collective-permute-start | bytes 98312 | tf_op jit(solution)/shard_map/ppermute | solution.py:566
  12.4 0.9 %select_reduce_fusion = s32[4]{0:T(128)S(1)} fusion(s32[4]{0:T(128)} %refs_4_.2, s32[4]{0:T(128)} %refs_2_.3, s32[4]{0:T(128)S(1)} %and_select_fusion), kind=kLoop, calls=%fused_computation.6 | loop fusion | flops 44 | bytes 64 | tf_op jit(solution)/shard_map/reduce_sum | solution.py:609
  13.2 0.1 fusion.1
  13.4 0.0 collective-permute-done.refs_1_
  13.4 0.2 collective-permute-done.1.refs_2_
  13.6 1.3 %collective-permute-done.2.refs_3_ = bf16[16,1024]{1,0:T(8,128)(2,1)S(1)} collective-permute-done((bf16[16,1024]{1,0:T(8,128)(2,1)S(1)}, bf16[16,1024]{1,0:T(8,128)(2,1)S(1)}, u32[]{:S(2)}, u32[]{:S(2)}) %collective-permute-start.2) | collective-permute-done | bytes 32800 | tf_op jit(solution)/shard_map/ppermute | solution.py:566
  14.9 0.9 %copy-done.3 = bf16[1,1024,128]{2,1,0:T(8,128)(2,1)S(1)} copy-done((bf16[1,1024,128]{2,1,0:T(8,128)(2,1)S(1)}, bf16[1,1024,128]{2,1,0:T(8,128)(2,1)}, u32[]{:S(2)}) %copy-start.3) | copy-done | bytes 262168
  15.9 0.2 rank_rows.1.refs_4_
  16.1 0.1 collective-permute-start.5
  16.1 1.6 %collective-permute-start.4 = (f32[32,128]{1,0:T(8,128)S(1)}, f32[32,128]{1,0:T(8,128)S(1)}, u32[]{:S(2)}, u32[]{:S(2)}) collective-permute-start(f32[32,128]{1,0:T(8,128)S(1)} %rank_rows.1.refs_4_), channel_id=1, source_target_pairs={{0,2},{1,3},{2,0},{3,1},{4,6},{5,7},{6,4},{7,5},{8,10},{9,11},{10,... | collective-permute-start | bytes 49160 | tf_op jit(solution)/shard_map/ppermute | solution.py:661
  17.7 0.3 collective-permute-start.3
  18.0 0.1 pad_maximum_fusion
  18.1 1.4 %collective-permute-done.5.refs_7_ = f32[32,128]{1,0:T(8,128)S(1)} collective-permute-done((f32[32,128]{1,0:T(8,128)S(1)}, f32[32,128]{1,0:T(8,128)S(1)}, u32[]{:S(2)}, u32[]{:S(2)}) %collective-permute-start.5) | collective-permute-done | bytes 16416 | tf_op jit(solution)/shard_map/ppermute | solution.py:661
  19.4 0.5 %collective-permute-done.4.refs_6_ = f32[32,128]{1,0:T(8,128)S(1)} collective-permute-done((f32[32,128]{1,0:T(8,128)S(1)}, f32[32,128]{1,0:T(8,128)S(1)}, u32[]{:S(2)}, u32[]{:S(2)}) %collective-permute-start.4) | collective-permute-done | bytes 16416 | tf_op jit(solution)/shard_map/ppermute | solution.py:661
  19.9 0.0 collective-permute-done.3.refs_5_
  19.9 0.9 %copy-done.2 = bf16[1,2,64,1024]{3,2,1,0:T(8,128)(2,1)S(1)} copy-done((bf16[1,2,64,1024]{3,2,1,0:T(8,128)(2,1)S(1)}, bf16[1,2,64,1024]{3,2,1,0:T(8,128)(2,1)}, u32[]{:S(2)}) %copy-start.2) | copy-done | bytes 262168
  20.9 0.3 query_rows.1
  21.2 0.3 collective-permute-start.6
  21.4 3.5 %collective-permute-start.7 = (bf16[40,1024]{1,0:T(8,128)(2,1)S(1)}, bf16[40,1024]{1,0:T(8,128)(2,1)S(1)}, u32[]{:S(2)}, u32[]{:S(2)}) collective-permute-start(bf16[40,1024]{1,0:T(8,128)(2,1)S(1)} %get-tuple-element.34), channel_id=1, source_target_pairs={{0,8},{4,12},{8,0},{12,4},{1,9},{5,13},{9,1},{13,5},{2,10},{6,14},... | collective-permute-start | bytes 245768 | tf_op jit(solution)/shard_map/ppermute | solution.py:566
  24.9 0.1 collective-permute-start.8
  25.0 0.8 %copy-done.6 = bf16[32,1024]{1,0:T(8,128)(2,1)S(1)} copy-done((bf16[32,1024]{1,0:T(8,128)(2,1)S(1)}, bf16[32,1024]{1,0:T(8,128)(2,1)}, u32[]{:S(2)}) %copy-start.6) | copy-done | bytes 65560
  25.9 0.8 %copy-done.7 = bf16[32,1024]{1,0:T(8,128)(2,1)S(1)} copy-done((bf16[32,1024]{1,0:T(8,128)(2,1)S(1)}, bf16[32,1024]{1,0:T(8,128)(2,1)}, u32[]{:S(2)}) %copy-start.7) | copy-done | bytes 65560
  26.7 0.7 %copy-done.9 = s32[4]{0:T(128)S(1)} copy-done((s32[4]{0:T(128)S(1)}, s32[4]{0:T(128)}, u32[]{:S(2)}) %copy-start.9) | copy-done | bytes 40
  27.4 0.7 %copy-done.10 = s32[4,4]{1,0:T(4,128)S(1)} copy-done((s32[4,4]{1,0:T(4,128)S(1)}, s32[4,4]{1,0:T(4,128)}, u32[]{:S(2)}) %copy-start.10) | copy-done | bytes 88
  28.1 0.7 %copy-done.12 = s32[32]{0:T(128)S(1)} copy-done((s32[32]{0:T(128)S(1)}, s32[32]{0:T(128)}, u32[]{:S(2)}) %copy-start.12) | copy-done | bytes 152
  28.7 0.7 %copy-done.13 = s32[4]{0:T(128)S(1)} copy-done((s32[4]{0:T(128)S(1)}, s32[4]{0:T(128)}, u32[]{:S(2)}) %copy-start.13) | copy-done | bytes 40
  29.4 1.8 %slot_tables.1 = (bf16[32,1024]{1,0:T(8,128)(2,1)}, bf16[32,1024]{1,0:T(8,128)(2,1)S(1)}, bf16[32,1024]{1,0:T(8,128)(2,1)S(1)}, bf16[32,32]{1,0:T(8,128)(2,1)S(1)}, s32[57]{0:T(128)S(1)}) custom-call(s32[32]{0:T(128)S(1)} %copy-done.12, s32[1]{0:T(128)S(6)} %copy.16.refs_1_, s32[4]{0:T(128)S(1)} %copy-done.9, s32[4,4]{1,0:T(4,128)S(1)} %copy-done.10, ...), custom_call_target="tpu_custom_call" | custom-call | tf_op jit(solution)/shard_map/slot_tables/pallas_call | solution.py:625
  31.2 0.0 collective-permute-done.6.refs_6_.refs_3_
  31.2 0.1 collective-permute-done.7.refs_7_.refs_4_
  31.3 0.0 collective-permute-done.8.refs_8_.refs_5_
  31.3 1.6 %copy-done = bf16[4,2,128,1024]{3,2,1,0:T(8,128)(2,1)S(1)} copy-done((bf16[4,2,128,1024]{3,2,1,0:T(8,128)(2,1)S(1)}, bf16[4,2,128,1024]{3,2,1,0:T(8,128)(2,1)}, u32[]{:S(2)}) %copy-start) | copy-done | bytes 2097176
  32.9 8.3 %prefix_attention.1 = (bf16[4,8,1152]{2,1,0:T(8,128)(2,1)S(1)}, bf16[4,8,1152]{2,1,0:T(8,128)(2,1)S(1)}, bf16[4,8,1152]{2,1,0:T(8,128)(2,1)S(1)}, bf16[4,8,1152]{2,1,0:T(8,128)(2,1)S(1)}) custom-call(s32[57]{0:T(128)S(1)} %get-tuple-element.24.refs_0_, bf16[4,2,128,1024]{3,2,1,0:T(8,128)(2,1)S(1)} %copy-done, ...), custom_call_target="tpu_custom_call" | custom-call | tf_op jit(solution)/shard_map/prefix_attention/pallas_call | solution.py:673
  41.2 2.2 %collective-permute-start.9 = (bf16[4,8,1152]{2,1,0:T(8,128)(2,1)S(1)}, bf16[4,8,1152]{2,1,0:T(8,128)(2,1)S(1)}, u32[]{:S(2)}, u32[]{:S(2)}) collective-permute-start(bf16[4,8,1152]{2,1,0:T(8,128)(2,1)S(1)} %get-tuple-element.40), channel_id=1, source_target_pairs={{0,4},{4,8},{8,12},{12,0},{1,5},{5,9},{9,13},{13,1},{2,6},{6,10},{... | collective-permute-start | bytes 221192 | tf_op jit(solution)/shard_map/ppermute | solution.py:566
  43.4 1.0 %collective-permute-start.10 = (bf16[4,8,1152]{2,1,0:T(8,128)(2,1)S(1)}, bf16[4,8,1152]{2,1,0:T(8,128)(2,1)S(1)}, u32[]{:S(2)}, u32[]{:S(2)}) collective-permute-start(bf16[4,8,1152]{2,1,0:T(8,128)(2,1)S(1)} %get-tuple-element.41), channel_id=1, source_target_pairs={{0,8},{4,12},{8,0},{12,4},{1,9},{5,13},{9,1},{13,5},{2,10},{6,14},... | collective-permute-start | bytes 221192 | tf_op jit(solution)/shard_map/ppermute | solution.py:566
  44.4 1.7 %collective-permute-start.11 = (bf16[4,8,1152]{2,1,0:T(8,128)(2,1)S(1)}, bf16[4,8,1152]{2,1,0:T(8,128)(2,1)S(1)}, u32[]{:S(2)}, u32[]{:S(2)}) collective-permute-start(bf16[4,8,1152]{2,1,0:T(8,128)(2,1)S(1)} %get-tuple-element.42), channel_id=1, source_target_pairs={{0,12},{4,0},{8,4},{12,8},{1,13},{5,1},{9,5},{13,9},{2,14},{6,2},{... | collective-permute-start | bytes 221192 | tf_op jit(solution)/shard_map/ppermute | solution.py:566
  46.2 2.3 %own_attention.1 = (bf16[32,1024]{1,0:T(8,128)(2,1)}, f32[32,1024]{1,0:T(8,128)S(1)}, f32[32,128]{1,0:T(8,128)S(1)}, f32[32,128]{1,0:T(8,128)S(1)}) custom-call(s32[57]{0:T(128)S(1)} %get-tuple-element.24.refs_0_, bf16[32,2,8,1024]{3,2,1,0:T(8,128)(2,1)S(1)} %copy-done.1, bf16[32,1024]{1,0:T(8,128)(2,1)S(1)} %get-tuple-element.26.refs_2_, ...), custom_call_target="tpu_custom_call" | custom-call | tf_op jit(solution)/shard_map/own_attention/pallas_call | solution.py:687
  48.4 0.0 collective-permute-done.9.refs_6_
  48.4 1.9 %collective-permute-done.10.refs_7_ = bf16[4,8,1152]{2,1,0:T(8,128)(2,1)S(1)} collective-permute-done((bf16[4,8,1152]{2,1,0:T(8,128)(2,1)S(1)}, bf16[4,8,1152]{2,1,0:T(8,128)(2,1)S(1)}, u32[]{:S(2)}, u32[]{:S(2)}) %collective-permute-start.10) | collective-permute-done | bytes 73760 | tf_op jit(solution)/shard_map/ppermute | solution.py:566
  50.4 0.0 collective-permute-done.11.refs_8_
  50.4 1.9 %combine.1 = bf16[32,1024]{1,0:T(8,128)(2,1)} custom-call(s32[57]{0:T(128)S(1)} %get-tuple-element.24.refs_0_, bf16[32,32]{1,0:T(8,128)(2,1)S(1)} %get-tuple-element.25.refs_4_.refs_1_, f32[32,1024]{1,0:T(8,128)S(1)} %get-tuple-element.36.refs_2_, f32[32,128]{1,0:T(8,128)S(1)} %get-tuple-element.37.refs_3_, f32[32,128]{1,0:T(8,128)S(1)} %get-tuple-element.38.refs_4_, ...), custom_call_target="tpu_custom_call" | custom-call | tf_op jit(solution)/shard_map/combine/pallas_call | solution.py:702
  (17 shorter events, 0.1 us)
Async XLA Ops:
  0.6 45.5 %copy-start.1 = (bf16[32,2,8,1024]{3,2,1,0:T(8,128)(2,1)S(1)}, bf16[32,2,8,1024]{3,2,1,0:T(8,128)(2,1)}, u32[]{:S(2)}) copy-start(bf16[32,2,8,1024]{3,2,1,0:T(8,128)(2,1)} %refs_1_.4) | copy-start | bytes 3145732
  1.4 0.8 %copy-start.4 = (bf16[32,1024]{1,0:T(8,128)(2,1)S(1)}, bf16[32,1024]{1,0:T(8,128)(2,1)}, u32[]{:S(2)}) copy-start(bf16[32,1024]{1,0:T(8,128)(2,1)} %refs_3_.3) | copy-start | bytes 196612
  2.2 0.8 %copy-start.5 = (bf16[32,1024]{1,0:T(8,128)(2,1)S(1)}, bf16[32,1024]{1,0:T(8,128)(2,1)}, u32[]{:S(2)}) copy-start(bf16[32,1024]{1,0:T(8,128)(2,1)} %refs_4_.3) | copy-start | bytes 196612
  3.1 0.7 %copy-start.8 = (s32[4]{0:T(128)S(1)}, s32[4]{0:T(128)}, u32[]{:S(2)}) copy-start(s32[4]{0:T(128)} %refs_2_.3) | copy-start | bytes 52
  3.7 0.7 %copy-start.11 = (s32[32]{0:T(128)S(1)}, s32[32]{0:T(128)}, u32[]{:S(2)}) copy-start(s32[32]{0:T(128)} %refs_0_.3) | copy-start | bytes 388
  5.3 8.0 %collective-permute-start = (bf16[16,1024]{1,0:T(8,128)(2,1)S(1)}, bf16[16,1024]{1,0:T(8,128)(2,1)S(1)}, u32[]{:S(2)}, u32[]{:S(2)}) collective-permute-start(bf16[16,1024]{1,0:T(8,128)(2,1)S(1)} %get-tuple-element.29), channel_id=1, source_target_pairs={{0,4},{4,8},{8,12},{12,0},{1,5},{5,9},{9,13},{13,1},{2,6},{6,10},{... | collective-permute-start | bytes 98312 | tf_op jit(solution)/shard_map/ppermute | solution.py:566
  8.4 5.2 %collective-permute-start.1 = (bf16[16,1024]{1,0:T(8,128)(2,1)S(1)}, bf16[16,1024]{1,0:T(8,128)(2,1)S(1)}, u32[]{:S(2)}, u32[]{:S(2)}) collective-permute-start(bf16[16,1024]{1,0:T(8,128)(2,1)S(1)} %get-tuple-element.30), channel_id=1, source_target_pairs={{0,8},{4,12},{8,0},{12,4},{1,9},{5,13},{9,1},{13,5},{2,10},{6,14},... | collective-permute-start | bytes 98312 | tf_op jit(solution)/shard_map/ppermute | solution.py:566
  11.0 3.9 %collective-permute-start.2 = (bf16[16,1024]{1,0:T(8,128)(2,1)S(1)}, bf16[16,1024]{1,0:T(8,128)(2,1)S(1)}, u32[]{:S(2)}, u32[]{:S(2)}) collective-permute-start(bf16[16,1024]{1,0:T(8,128)(2,1)S(1)} %get-tuple-element.31), channel_id=1, source_target_pairs={{0,12},{4,0},{8,4},{12,8},{1,13},{5,1},{9,5},{13,9},{2,14},{6,2},{... | collective-permute-start | bytes 98312 | tf_op jit(solution)/shard_map/ppermute | solution.py:566
  14.9 1.0 %copy-start.3 = (bf16[1,1024,128]{2,1,0:T(8,128)(2,1)S(1)}, bf16[1,1024,128]{2,1,0:T(8,128)(2,1)}, u32[]{:S(2)}) copy-start(bf16[1,1024,128]{2,1,0:T(8,128)(2,1)} %param.17) | copy-start | bytes 786436
  16.1 3.4 %collective-permute-start.5 = (f32[32,128]{1,0:T(8,128)S(1)}, f32[32,128]{1,0:T(8,128)S(1)}, u32[]{:S(2)}, u32[]{:S(2)}) collective-permute-start(f32[32,128]{1,0:T(8,128)S(1)} %rank_rows.1.refs_4_), channel_id=1, source_target_pairs={{0,3},{1,2},{2,1},{3,0},{4,7},{5,6},{6,5},{7,4},{8,11},{9,10},{10,... | collective-permute-start | bytes 49160 | tf_op jit(solution)/shard_map/ppermute | solution.py:661
  16.1 3.8 %collective-permute-start.4 = (f32[32,128]{1,0:T(8,128)S(1)}, f32[32,128]{1,0:T(8,128)S(1)}, u32[]{:S(2)}, u32[]{:S(2)}) collective-permute-start(f32[32,128]{1,0:T(8,128)S(1)} %rank_rows.1.refs_4_), channel_id=1, source_target_pairs={{0,2},{1,3},{2,0},{3,1},{4,6},{5,7},{6,4},{7,5},{8,10},{9,11},{10,... | collective-permute-start | bytes 49160 | tf_op jit(solution)/shard_map/ppermute | solution.py:661
  17.7 2.3 %collective-permute-start.3 = (f32[32,128]{1,0:T(8,128)S(1)}, f32[32,128]{1,0:T(8,128)S(1)}, u32[]{:S(2)}, u32[]{:S(2)}) collective-permute-start(f32[32,128]{1,0:T(8,128)S(1)} %rank_rows.1.refs_4_), channel_id=1, source_target_pairs={{0,1},{1,0},{2,3},{3,2},{4,5},{5,4},{6,7},{7,6},{8,9},{9,8},{10,11... | collective-permute-start | bytes 49160 | tf_op jit(solution)/shard_map/ppermute | solution.py:661
  19.9 1.0 %copy-start.2 = (bf16[1,2,64,1024]{3,2,1,0:T(8,128)(2,1)S(1)}, bf16[1,2,64,1024]{3,2,1,0:T(8,128)(2,1)}, u32[]{:S(2)}) copy-start(bf16[1,2,64,1024]{3,2,1,0:T(8,128)(2,1)} %param.18) | copy-start | bytes 786436
  21.2 10.1 %collective-permute-start.6 = (bf16[40,1024]{1,0:T(8,128)(2,1)S(1)}, bf16[40,1024]{1,0:T(8,128)(2,1)S(1)}, u32[]{:S(2)}, u32[]{:S(2)}) collective-permute-start(bf16[40,1024]{1,0:T(8,128)(2,1)S(1)} %get-tuple-element.33), channel_id=1, source_target_pairs={{0,4},{4,8},{8,12},{12,0},{1,5},{5,9},{9,13},{13,1},{2,6},{6,10},{... | collective-permute-start | bytes 245768 | tf_op jit(solution)/shard_map/ppermute | solution.py:566
  21.4 9.9 %collective-permute-start.7 = (bf16[40,1024]{1,0:T(8,128)(2,1)S(1)}, bf16[40,1024]{1,0:T(8,128)(2,1)S(1)}, u32[]{:S(2)}, u32[]{:S(2)}) collective-permute-start(bf16[40,1024]{1,0:T(8,128)(2,1)S(1)} %get-tuple-element.34), channel_id=1, source_target_pairs={{0,8},{4,12},{8,0},{12,4},{1,9},{5,13},{9,1},{13,5},{2,10},{6,14},... | collective-permute-start | bytes 245768 | tf_op jit(solution)/shard_map/ppermute | solution.py:566
  24.9 6.4 %collective-permute-start.8 = (bf16[40,1024]{1,0:T(8,128)(2,1)S(1)}, bf16[40,1024]{1,0:T(8,128)(2,1)S(1)}, u32[]{:S(2)}, u32[]{:S(2)}) collective-permute-start(bf16[40,1024]{1,0:T(8,128)(2,1)S(1)} %get-tuple-element.35), channel_id=1, source_target_pairs={{0,12},{4,0},{8,4},{12,8},{1,13},{5,1},{9,5},{13,9},{2,14},{6,2},{... | collective-permute-start | bytes 245768 | tf_op jit(solution)/shard_map/ppermute | solution.py:566
  25.0 0.8 %copy-start.6 = (bf16[32,1024]{1,0:T(8,128)(2,1)S(1)}, bf16[32,1024]{1,0:T(8,128)(2,1)}, u32[]{:S(2)}) copy-start(bf16[32,1024]{1,0:T(8,128)(2,1)} %refs_5_.1) | copy-start | bytes 196612
  25.9 0.8 %copy-start.7 = (bf16[32,1024]{1,0:T(8,128)(2,1)S(1)}, bf16[32,1024]{1,0:T(8,128)(2,1)}, u32[]{:S(2)}) copy-start(bf16[32,1024]{1,0:T(8,128)(2,1)} %refs_6_.1) | copy-start | bytes 196612
  26.7 0.7 %copy-start.9 = (s32[4]{0:T(128)S(1)}, s32[4]{0:T(128)}, u32[]{:S(2)}) copy-start(s32[4]{0:T(128)} %refs_2_.3) | copy-start | bytes 52
  27.4 0.7 %copy-start.10 = (s32[4,4]{1,0:T(4,128)S(1)}, s32[4,4]{1,0:T(4,128)}, u32[]{:S(2)}) copy-start(s32[4,4]{1,0:T(4,128)} %refs_3_.2) | copy-start | bytes 196
  28.1 0.7 %copy-start.12 = (s32[32]{0:T(128)S(1)}, s32[32]{0:T(128)}, u32[]{:S(2)}) copy-start(s32[32]{0:T(128)} %refs_0_.3) | copy-start | bytes 388
  28.7 0.7 %copy-start.13 = (s32[4]{0:T(128)S(1)}, s32[4]{0:T(128)}, u32[]{:S(2)}) copy-start(s32[4]{0:T(128)} %refs_4_.2) | copy-start | bytes 52
  31.3 1.6 %copy-start = (bf16[4,2,128,1024]{3,2,1,0:T(8,128)(2,1)S(1)}, bf16[4,2,128,1024]{3,2,1,0:T(8,128)(2,1)}, u32[]{:S(2)}) copy-start(bf16[4,2,128,1024]{3,2,1,0:T(8,128)(2,1)} %refs_1_.5) | copy-start | bytes 6291460
  41.2 7.2 %collective-permute-start.9 = (bf16[4,8,1152]{2,1,0:T(8,128)(2,1)S(1)}, bf16[4,8,1152]{2,1,0:T(8,128)(2,1)S(1)}, u32[]{:S(2)}, u32[]{:S(2)}) collective-permute-start(bf16[4,8,1152]{2,1,0:T(8,128)(2,1)S(1)} %get-tuple-element.40), channel_id=1, source_target_pairs={{0,4},{4,8},{8,12},{12,0},{1,5},{5,9},{9,13},{13,1},{2,6},{6,10},{... | collective-permute-start | bytes 221192 | tf_op jit(solution)/shard_map/ppermute | solution.py:566
  43.4 7.0 %collective-permute-start.10 = (bf16[4,8,1152]{2,1,0:T(8,128)(2,1)S(1)}, bf16[4,8,1152]{2,1,0:T(8,128)(2,1)S(1)}, u32[]{:S(2)}, u32[]{:S(2)}) collective-permute-start(bf16[4,8,1152]{2,1,0:T(8,128)(2,1)S(1)} %get-tuple-element.41), channel_id=1, source_target_pairs={{0,8},{4,12},{8,0},{12,4},{1,9},{5,13},{9,1},{13,5},{2,10},{6,14},... | collective-permute-start | bytes 221192 | tf_op jit(solution)/shard_map/ppermute | solution.py:566
  44.4 6.0 %collective-permute-start.11 = (bf16[4,8,1152]{2,1,0:T(8,128)(2,1)S(1)}, bf16[4,8,1152]{2,1,0:T(8,128)(2,1)S(1)}, u32[]{:S(2)}, u32[]{:S(2)}) collective-permute-start(bf16[4,8,1152]{2,1,0:T(8,128)(2,1)S(1)} %get-tuple-element.42), channel_id=1, source_target_pairs={{0,12},{4,0},{8,4},{12,8},{1,13},{5,1},{9,5},{13,9},{2,14},{6,2},{... | collective-permute-start | bytes 221192 | tf_op jit(solution)/shard_map/ppermute | solution.py:566
